TPU v7x, 512 devices: a whole 4x4x16 slice. The times are simulated.
512 devices in a mesh: dp: 64 (over z, y), feat: 8 (over x, core).
Axes of the slice: x: 4, y: 4, z: 16, core: 2. Of those that a mesh axis runs over, the one named last changes fastest.
Arguments:
- points: float32 [65536, 256], P('dp'), may hold values from -6 to 6
- frequencies: float32 [256, 1024], P(None, 'feat'), may hold values from -0.5 to 0.5
- halton_start: int32 [1], replicated, may hold values from 0 to 39999
Outputs:
- scores: float32 [65536], P(('dp', 'feat'))
- r_factor: float32 [1024, 1024], P(None, 'feat')
All inputs are finite; a program needn't handle non-finite values.
Results may differ from a plain program's by a relative error of at most 0.0003.
Values sent between devices are 32-bit elements; how exact they have to be, the bound alone decides.
A program may use at most 64 MiB of HBM per device.

v0:
```python
import math

import jax
import jax.numpy as jnp
from jax import lax
from jax.sharding import PartitionSpec as P

ridge_level = 0.1


def halton_phase(halton_start, columns):
    index_value = halton_start[0] + columns
    radical = jnp.zeros(columns.shape, jnp.float32)
    for place in range(16):
        digit_bit = index_value // (1 << place) % 2
        radical = radical + digit_bit.astype(jnp.float32) * 0.5 ** (place + 1)
    return 2.0 * math.pi * radical


def featurize(row_block, frequencies, phase):
    angles = jnp.dot(
        row_block, frequencies, precision=lax.Precision.HIGHEST, preferred_element_type=jnp.float32
    )
    return math.sqrt(2.0) * jnp.cos(angles + phase)


def per_device(points, frequencies, halton_start):
    panel_width = frequencies.shape[1]
    feat_count = lax.axis_size("feat")
    group_count = lax.axis_size("dp")
    feat_total = panel_width * feat_count
    row_count = points.shape[0]
    total_rows = row_count * group_count
    feat_place = lax.axis_index("feat")
    columns = feat_place * panel_width + jnp.arange(panel_width, dtype=jnp.int32)
    own_panel = featurize(points, frequencies, halton_phase(halton_start, columns))
    gram_block = jnp.dot(
        lax.all_gather(own_panel, "feat", axis=1, tiled=True).T,
        own_panel,
        precision=lax.Precision.HIGHEST,
        preferred_element_type=jnp.float32,
    )
    own_rows = lax.all_to_all(own_panel, "feat", split_axis=0, concat_axis=1, tiled=True)
    summed = lax.psum(gram_block, "dp")
    gram_total = lax.all_gather(summed, "feat", axis=1, tiled=True)
    gram_full = gram_total / total_rows + ridge_level * jnp.eye(feat_total, dtype=jnp.float32)
    factor = jnp.linalg.cholesky(gram_full)
    solved = lax.linalg.triangular_solve(factor, own_rows.T, left_side=True, lower=True)
    scores = jnp.sum(solved * solved, axis=0) / feat_total
    own_factor = lax.dynamic_slice_in_dim(factor, feat_place * panel_width, panel_width, 1)
    return (scores, own_factor)


def solution(mesh):
    in_specs = (P("dp", None), P(None, "feat"), P())
    out_specs = (P(("dp", "feat")), P(None, "feat"))
    return jax.shard_map(
        per_device, mesh=mesh, in_specs=in_specs, out_specs=out_specs, check_vma=False
    )
```

profile of v0, /device:TPU:1, one launch (start us, length us, event | category | flops | bytes accessed | tf_op | source)
XLA Modules:
  0.0 727.1 jit_solution(13208123939911550002)
XLA Ops:
  12.8 49.5 %all-gather.3.cloned.1.call-done = f32[1024,1024]{1,0:T(8,128)} async-done(((f32[1024,128]{1,0:T(8,128)}), f32[1024,1024]{1,0:T(8,128)}) %all-gather.3.cloned.1.call-update) | async-done | bytes 4194320 | tf_op jit(solution)/shard_map/all_gather | solution.py:38
  62.3 5.6 fusion.128
  68.0 256.7 %all-reduce.3.cloned.1.call-done = f32[1024,128]{0,1:T(8,128)} async-done(((f32[1024,128]{0,1:T(8,128)}), f32[1024,128]{0,1:T(8,128)}) %all-reduce.3.cloned.1.call-update) | async-done | bytes 524304 | tf_op jit(solution)/shard_map/psum | solution.py:44
  325.7 15.0 %all-to-all-start = ((f32[8,128,128]{1,2,0:T(8,128)}), f32[8,128,128]{1,2,0:T(8,128)S(1)}, u32[]{:S(2)}, u32[]{:S(2)}) async-start(f32[8,128,128]{1,2,0:T(8,128)} %copy.42), calls=%async_computation | async-start | bytes 1048576 | tf_op jit(solution)/shard_map/all_to_all | solution.py:43
  340.7 31.0 %all-gather.5.cloned.1.call-done = f32[1024,1024]{0,1:T(8,128)} async-done(((f32[1024,128]{0,1:T(8,128)}), f32[1024,1024]{0,1:T(8,128)}) %all-gather.5.cloned.1.call-update) | async-done | bytes 4194320 | tf_op jit(solution)/shard_map/all_gather | solution.py:45
  376.7 5.8 copy.25
  388.9 11.7 %cholesky.222 = f32[128,128]{1,0:T(8,128)S(1)} custom-call(f32[128,128]{1,0:T(8,128)S(1)} %cholesky.577), custom_call_target="Cholesky" | custom-call | tf_op jit(solution)/shard_map/jit(cholesky)/cholesky | solution.py:47
  400.8 9.8 %custom-call.62 = f32[1,128,128]{1,2,0:T(8,128)S(1)} custom-call(f32[1,128,128]{2,1,0:T(8,128)S(1)} %get-tuple-element.72), custom_call_target="InvertDiagBlocksLowerTriangular" | custom-call | tf_op jit(solution)/shard_map/jit(cholesky)/cholesky | solution.py:47
  413.9 11.7 %cholesky.243 = f32[128,128]{1,0:T(8,128)S(1)} custom-call(f32[128,128]{1,0:T(8,128)S(1)} %cholesky.581), custom_call_target="Cholesky" | custom-call | tf_op jit(solution)/shard_map/jit(cholesky)/cholesky | solution.py:47
  425.9 9.8 %custom-call.63 = f32[1,128,128]{1,2,0:T(8,128)S(1)} custom-call(f32[1,128,128]{2,1,0:T(8,128)S(1)} %get-tuple-element.70), custom_call_target="InvertDiagBlocksLowerTriangular" | custom-call | tf_op jit(solution)/shard_map/jit(cholesky)/cholesky | solution.py:47
  441.3 11.7 %cholesky.466 = f32[128,128]{1,0:T(8,128)S(1)} custom-call(f32[128,128]{1,0:T(8,128)S(1)} %cholesky.586), custom_call_target="Cholesky" | custom-call | tf_op jit(solution)/shard_map/jit(cholesky)/cholesky | solution.py:47
  453.7 9.8 %custom-call.64 = f32[1,128,128]{1,2,0:T(8,128)S(1)} custom-call(f32[1,128,128]{2,1,0:T(8,128)S(1)} %get-tuple-element.68), custom_call_target="InvertDiagBlocksLowerTriangular" | custom-call | tf_op jit(solution)/shard_map/jit(cholesky)/cholesky | solution.py:47
  468.1 11.7 %cholesky.485 = f32[128,128]{1,0:T(8,128)S(1)} custom-call(f32[128,128]{1,0:T(8,128)S(1)} %cholesky.591), custom_call_target="Cholesky" | custom-call | tf_op jit(solution)/shard_map/jit(cholesky)/cholesky | solution.py:47
  480.6 9.8 %custom-call.65 = f32[1,128,128]{1,2,0:T(8,128)S(1)} custom-call(f32[1,128,128]{2,1,0:T(8,128)S(1)} %get-tuple-element.66), custom_call_target="InvertDiagBlocksLowerTriangular" | custom-call | tf_op jit(solution)/shard_map/jit(cholesky)/cholesky | solution.py:47
  494.7 12.1 %cholesky.504 = f32[128,128]{1,0:T(8,128)S(1)} custom-call(f32[128,128]{1,0:T(8,128)S(1)} %cholesky.596), custom_call_target="Cholesky" | custom-call | tf_op jit(solution)/shard_map/jit(cholesky)/cholesky | solution.py:47
  507.6 9.8 %custom-call.66 = f32[1,128,128]{1,2,0:T(8,128)S(1)} custom-call(f32[1,128,128]{2,1,0:T(8,128)S(1)} %get-tuple-element.64), custom_call_target="InvertDiagBlocksLowerTriangular" | custom-call | tf_op jit(solution)/shard_map/jit(cholesky)/cholesky | solution.py:47
  521.8 11.7 %cholesky.524 = f32[128,128]{1,0:T(8,128)S(1)} custom-call(f32[128,128]{1,0:T(8,128)S(1)} %cholesky.601), custom_call_target="Cholesky" | custom-call | tf_op jit(solution)/shard_map/jit(cholesky)/cholesky | solution.py:47
  534.3 9.8 %custom-call.67 = f32[1,128,128]{1,2,0:T(8,128)S(1)} custom-call(f32[1,128,128]{2,1,0:T(8,128)S(1)} %get-tuple-element.62), custom_call_target="InvertDiagBlocksLowerTriangular" | custom-call | tf_op jit(solution)/shard_map/jit(cholesky)/cholesky | solution.py:47
  548.0 11.7 %cholesky.544 = f32[128,128]{1,0:T(8,128)S(1)} custom-call(f32[128,128]{1,0:T(8,128)S(1)} %cholesky.606), custom_call_target="Cholesky" | custom-call | tf_op jit(solution)/shard_map/jit(cholesky)/cholesky | solution.py:47
  560.5 9.8 %custom-call.68 = f32[1,128,128]{1,2,0:T(8,128)S(1)} custom-call(f32[1,128,128]{2,1,0:T(8,128)S(1)} %get-tuple-element.60), custom_call_target="InvertDiagBlocksLowerTriangular" | custom-call | tf_op jit(solution)/shard_map/jit(cholesky)/cholesky | solution.py:47
  573.4 11.7 %cholesky.562 = f32[128,128]{1,0:T(8,128)S(1)} custom-call(f32[128,128]{1,0:T(8,128)S(1)} %convolution_subtract_fusion.11), custom_call_target="Cholesky" | custom-call | tf_op jit(solution)/shard_map/jit(cholesky)/cholesky | solution.py:47
  595.7 6.6 fusion.1
  602.2 23.6 %while.1 = (s32[]{:T(128)}, f32[1024,1024]{0,1:T(8,128)}, s32[8,2]{0,1:T(2,128)S(1)}, f32[8,128,128]{2,1,0:T(8,128)S(1)}, s32[]{:T(128)}) while((s32[]{:T(128)}, f32[1024,1024]{0,1:T(8,128)}, s32[8,2]{0,1:T(2,128)S(1)}, f32[8,128,128]{2,1,0:T(8,128)S(1)}, s32[]{:T(128)}) %tuple.58), condition=%wide.while_cond, body=%wide.while_body.sunk | while | flops 2 | bytes 393329 | solution.py:48
  625.8 78.6 %custom-call.69 = f32[8,128,128]{1,2,0:T(8,128)S(1)} custom-call(f32[8,128,128]{2,1,0:T(8,128)S(1)} %get-tuple-element.9), custom_call_target="InvertDiagBlocksLowerTriangular" | custom-call | tf_op jit(solution)/shard_map/triangular_solve | solution.py:48
  (136 shorter events, 95.0 us)
Async XLA Ops:
  7.2 1.2 copy-start
  7.2 55.1 %all-gather.3.cloned.1.call-start = ((), (), s32[]{:S(2)}) async-start(), calls=%async_computation.1 | async-start | bytes 4718592 | tf_op jit(solution)/shard_map/all_gather | solution.py:38
  12.7 312.0 %copy-start.3 = (f32[1024,128]{1,0:T(8,128)S(1)}, f32[1024,128]{1,0:T(8,128)}, u32[]{:S(2)}) copy-start(f32[1024,128]{1,0:T(8,128)} %fusion.3) | copy-start | bytes 1572868
  12.7 312.0 %all-reduce.3.cloned.1.call-start = ((), (), s32[]{:S(2)}) async-start(), calls=%async_computation.2 | async-start | bytes 1048576 | tf_op jit(solution)/shard_map/psum | solution.py:44
  68.0 303.7 %all-gather.5.cloned.1.call-start = ((), (), s32[]{:S(2)}) async-start(), calls=%async_computation.3 | async-start | bytes 4718592 | tf_op jit(solution)/shard_map/all_gather | solution.py:45
  325.7 378.7 %all-to-all-start = ((f32[8,128,128]{1,2,0:T(8,128)}), f32[8,128,128]{1,2,0:T(8,128)S(1)}, u32[]{:S(2)}, u32[]{:S(2)}) async-start(f32[8,128,128]{1,2,0:T(8,128)} %copy.42), calls=%async_computation | async-start | bytes 1048576 | tf_op jit(solution)/shard_map/all_to_all | solution.py:43
  387.0 1.9 copy-start.2
  436.8 2.0 copy-start.1
Sparse Core Ops, SparseCore 0:
  12.8 49.4 all-gather.2
  68.1 256.5 all-reduce.2
  327.1 44.5 all-gather.4
where the time goes:
time: 733 us; the launch traced here: 727 us
  waiting for transfers between devices  337 us (46%)
  other arithmetic  263 us (36%)
  matrix products  49.2 us (7%)
  local copies, waits for them, and re-layouts  41.8 us (6%)
  between operations  20.1 us (3%)
  starting transfers between devices  15.1 us (2%)
    psum x1, waiting for transfers between devices, per_device(): summed = lax.psum(gram_block, 'dp')  257 us
    another operation x30, other arithmetic, per_device(): factor = jnp.linalg.cholesky(gram_full)  168 us
    another operation x3, other arithmetic, per_device(): lax.linalg.triangular_solve(factor, own_rows.T, left_side=True, lower=True)  85.2 us
    all_gather x1, waiting for transfers between devices, per_device(): lax.all_gather(own_panel, 'feat', axis=1, tiled=True)  49.5 us
    all_gather x1, waiting for transfers between devices, per_device(): gram_total = lax.all_gather(summed, 'feat', axis=1, tiled=True)  31 us
    another operation x14, matrix products, per_device(): factor = jnp.linalg.cholesky(gram_full)  26.2 us
    another operation x40, local copies, waits for them, and re-layouts  23.1 us
    all_to_all x1, starting transfers between devices, per_device(): lax.all_to_all(own_panel, 'feat', split_axis=0, concat_axis=1, tiled=True)  15 us
  transfers between devices with their start and end apart: 4, of which 3 were waited for; matrix products, arithmetic and copies ran while one was open for 45% of the time, Pallas kernels for 0%

commit v1 on v0

--- a/solution.py
+++ b/solution.py
@@ -3,9 +3,134 @@
 import jax
 import jax.numpy as jnp
 from jax import lax
+from jax.experimental import pallas as pl
+from jax.experimental.pallas import tpu as pltpu
 from jax.sharding import PartitionSpec as P
 
 ridge_level = 0.1
+
+
+HI = lax.Precision.HIGHEST
+
+
+def spread_row(tile, place):
+    return jnp.broadcast_to(tile[place : place + 1, :], (8, 128))
+
+
+def gram_of(left, right):
+    return lax.dot_general(
+        left, right, (((0,), (0,)), ((), ())), precision=HI, preferred_element_type=jnp.float32
+    )
+
+
+def eliminate(tiles, first, width):
+    row = lax.broadcasted_iota(jnp.int32, (8, 128), 0)
+    depth = width // 8
+    column = [[None] * depth for _ in range(width)]
+    for k in range(width):
+        for i in range(k // 8, depth):
+            column[k][i] = jnp.broadcast_to(tiles[i][0][:, first + k : first + k + 1], (8, 128))
+    pivots = [jnp.ones((8, 128), jnp.float32) for _ in range(depth)]
+    for k in range(width):
+        kt, ks = k // 8, k % 8
+        pivot = spread_row(column[k][kt], ks)
+        pivots[kt] = jnp.where(row == ks, pivot, pivots[kt])
+        if k == width - 1:
+            break
+        inverse = 1.0 / pivot
+        weight = {i: column[k][i] * inverse for i in range(kt, depth)}
+        weight[kt] = jnp.where(row > ks, weight[kt], 0.0)
+        for m in range(k + 1, width):
+            x = spread_row(column[k][m // 8], m % 8)
+            for i in range(m // 8, depth):
+                column[m][i] = column[m][i] - weight[i] * x
+        for c in range(len(tiles[0])):
+            t = spread_row(tiles[kt][c], ks)
+            for i in range(kt + (ks == 7), depth):
+                tiles[i][c] = tiles[i][c] - weight[i] * t
+    for i in range(depth):
+        scale = lax.rsqrt(pivots[i])
+        tiles[i] = [t * scale for t in tiles[i]]
+    return tiles
+
+
+def factor_diagonal(work, width):
+    for s in range(128 // width):
+        first = s * width
+        block = work[first : first + width, :]
+        if s:
+            above = work[0:first, :]
+            block = block - gram_of(above[:, first : first + width], above)
+        tiles = [
+            [block[8 * i : 8 * i + 8, 128 * c : 128 * c + 128] for c in range(2)]
+            for i in range(width // 8)
+        ]
+        tiles = eliminate(tiles, first, width)
+        for i in range(width // 8):
+            for c in range(2):
+                work[first + 8 * i : first + 8 * i + 8, 128 * c : 128 * c + 128] = tiles[i][c]
+
+
+def factor_kernel(gram_ref, rows_ref, factor_ref, score_ref, a_ref, work):
+    total = gram_ref.shape[0]
+    blocks = total // 128
+    a_ref[:, 0:total] = gram_ref[...]
+    a_ref[:, total : total + 128] = rows_ref[...]
+    eye = (
+        lax.broadcasted_iota(jnp.int32, (128, 128), 0)
+        == lax.broadcasted_iota(jnp.int32, (128, 128), 1)
+    ).astype(jnp.float32)
+
+    @pl.loop(0, blocks)
+    def _(p):
+        r = pl.multiple_of(p * 128, 128)
+        work[:, 0:128] = a_ref[pl.ds(r, 128), pl.ds(r, 128)]
+        work[:, 128:256] = eye
+        factor_diagonal(work, 32)
+        a_ref[pl.ds(r, 128), :] = jnp.dot(
+            work[:, 128:256],
+            a_ref[pl.ds(r, 128), :],
+            precision=HI,
+            preferred_element_type=jnp.float32,
+        )
+
+        @pl.loop(p + 1, blocks)
+        def _(i):
+            ri = pl.multiple_of(i * 128, 128)
+            a_ref[pl.ds(ri, 128), :] -= gram_of(
+                a_ref[pl.ds(r, 128), pl.ds(ri, 128)], a_ref[pl.ds(r, 128), :]
+            )
+
+        a_ref[pl.ds(r, 128), pl.ds(r, 128)] = work[:, 0:128]
+
+    solved = a_ref[:, total : total + 128]
+    score_ref[...] = jnp.sum(solved * solved, axis=0, keepdims=True) / total
+    place = lax.axis_index("feat")
+    mine = pl.multiple_of(place * 128, 128)
+    for b in range(blocks):
+        piece = a_ref[pl.ds(mine, 128), 128 * b : 128 * b + 128].T
+        below = 128 * b + lax.broadcasted_iota(jnp.int32, (128, 128), 0)
+        across = mine + lax.broadcasted_iota(jnp.int32, (128, 128), 1)
+        factor_ref[128 * b : 128 * b + 128, :] = jnp.where(below >= across, piece, 0.0)
+
+
+def factor_and_score(gram_full, rows):
+    total = gram_full.shape[0]
+    in_vmem = pl.BlockSpec(memory_space=pltpu.VMEM)
+    return pl.pallas_call(
+        factor_kernel,
+        out_shape=(
+            jax.ShapeDtypeStruct((total, 128), jnp.float32),
+            jax.ShapeDtypeStruct((1, 128), jnp.float32),
+        ),
+        in_specs=[in_vmem] * 2,
+        out_specs=(in_vmem,) * 2,
+        scratch_shapes=[
+            pltpu.VMEM((total, total + 128), jnp.float32),
+            pltpu.VMEM((128, 256), jnp.float32),
+        ],
+        compiler_params=pltpu.CompilerParams(vmem_limit_bytes=48 * 2**20),
+    )(gram_full, rows)
 
 
 def halton_phase(halton_start, columns):
@@ -44,11 +169,8 @@
     summed = lax.psum(gram_block, "dp")
     gram_total = lax.all_gather(summed, "feat", axis=1, tiled=True)
     gram_full = gram_total / total_rows + ridge_level * jnp.eye(feat_total, dtype=jnp.float32)
-    factor = jnp.linalg.cholesky(gram_full)
-    solved = lax.linalg.triangular_solve(factor, own_rows.T, left_side=True, lower=True)
-    scores = jnp.sum(solved * solved, axis=0) / feat_total
-    own_factor = lax.dynamic_slice_in_dim(factor, feat_place * panel_width, panel_width, 1)
-    return (scores, own_factor)
+    own_factor, scores = factor_and_score(gram_full, own_rows.T)
+    return (scores.reshape(128), own_factor)
 
 
 def solution(mesh):

time: 733 us -> 446 us (0.61)
  other arithmetic: 263 us -> 5.08 us
  Pallas kernels: 0 us -> 51.8 us
  local copies, waits for them, and re-layouts: 41.8 us -> 3.58 us
  matrix products: 49.2 us -> 14 us
    another operation x33 -> x0, other arithmetic: 253 us -> none  [the longest x30 168 us: per_device(): factor = jnp.linalg.cholesky(gram_full)]
    pallas_call x0 -> x1, Pallas kernels: none -> 51.8 us  [factor_and_score(): pl.pallas_call(factor_kernel, out_shape=(jax.ShapeDtypeStruct((total, 128...]
    another operation x29 -> x0, matrix products: 39.3 us -> none  [the longest x14 26.2 us: per_device(): factor = jnp.linalg.cholesky(gram_full)]
    another operation x66 -> x0, local copies, waits for them, and re-layouts: 28.7 us -> none
  transfers between devices with their start and end apart: 4 -> 4, of which waited for: 3 -> 3; matrix products, arithmetic and copies ran while one was open for 45% -> 1% of each run, Pallas kernels for 0% -> 0%
where the time goes in v1:
time: 446 us; the launch traced here: 445 us
  waiting for transfers between devices  341 us (76%)
  Pallas kernels  51.8 us (12%)
  starting transfers between devices  15.1 us (3%)
  between operations  14.5 us (3%)
  matrix products  14 us (3%)
  other arithmetic  5.08 us (1%)
    psum x1, waiting for transfers between devices, per_device(): summed = lax.psum(gram_block, 'dp')  257 us
    pallas_call x1, Pallas kernels, factor_and_score(): pl.pallas_call(factor_kernel, out_shape=(jax.ShapeDtypeStruct((total, 128...  51.8 us
    all_gather x1, waiting for transfers between devices, per_device(): lax.all_gather(own_panel, 'feat', axis=1, tiled=True)  49.5 us
    all_gather x1, waiting for transfers between devices, per_device(): gram_total = lax.all_gather(summed, 'feat', axis=1, tiled=True)  34.9 us
    all_to_all x1, starting transfers between devices, per_device(): lax.all_to_all(own_panel, 'feat', split_axis=0, concat_axis=1, tiled=True)  15 us
    dot_general x1, matrix products, per_device(): jnp.dot(lax.all_gather(own_panel, 'feat', axis=1, tiled=True).T, own_pane...  9.76 us
  transfers between devices with their start and end apart: 4, of which 3 were waited for; matrix products, arithmetic and copies ran while one was open for 1% of the time, Pallas kernels for 0%

profile of v1, /device:TPU:1, one launch (start us, length us, event | category | flops | bytes accessed | tf_op | source)
XLA Modules:
  0.0 445.3 jit_solution(1645098428372900788)
XLA Ops:
  7.2 0.0 copy-start
  7.2 0.0 all-gather.3.cloned.1.call-start
  8.0 0.1 fusion.64
  8.0 0.4 copy-done
  8.4 4.3 fusion.1
  12.7 0.0 copy-start.2
  12.7 0.0 all-gather.3.cloned.1.call-update
  12.7 0.0 all-reduce.2.cloned.1.call-start
  12.8 49.5 %all-gather.3.cloned.1.call-done = f32[1024,1024]{1,0:T(8,128)} async-done(((f32[1024,128]{1,0:T(8,128)}), f32[1024,1024]{1,0:T(8,128)}) %all-gather.3.cloned.1.call-update) | async-done | bytes 4194320 | tf_op jit(solution)/shard_map/all_gather | solution.py:163
  62.3 9.8 %fusion.65 = f32[1024,128]{1,0:T(8,128)} fusion(f32[1024,1024]{1,0:T(8,128)} %all-gather.3.cloned.1.call-done, f32[1024,128]{1,0:T(8,128)} %fusion.1), kind=kOutput, calls=%fused_computation.161 | convolution fusion | flops 1610612736 | bytes 5242880 | tf_op jit(solution)/shard_map/dot_general | solution.py:162
  72.1 0.0 all-reduce.2.cloned.1.call-update
  72.1 0.0 all-gather.5.cloned.1.call-start
  72.1 256.7 %all-reduce.2.cloned.1.call-done = f32[1024,128]{1,0:T(8,128)} async-done(((f32[1024,128]{1,0:T(8,128)}), f32[1024,128]{1,0:T(8,128)}) %all-reduce.2.cloned.1.call-update) | async-done | bytes 524304 | tf_op jit(solution)/shard_map/psum | solution.py:169
  328.8 0.0 all-gather.5.cloned.1.call-update
  328.8 0.0 copy-done.2
  328.8 1.0 copy.5
  329.8 15.0 %all-to-all-start = ((f32[8,128,128]{1,2,0:T(8,128)}), f32[8,128,128]{1,2,0:T(8,128)S(1)}, u32[]{:S(2)}, u32[]{:S(2)}) async-start(f32[8,128,128]{1,2,0:T(8,128)} %copy.5), calls=%async_computation | async-start | bytes 1048576 | tf_op jit(solution)/shard_map/all_to_all | solution.py:168
  344.8 34.9 %all-gather.5.cloned.1.call-done = f32[1024,1024]{1,0:T(8,128)} async-done(((f32[1024,128]{1,0:T(8,128)}), f32[1024,1024]{1,0:T(8,128)}) %all-gather.5.cloned.1.call-update) | async-done | bytes 4194320 | tf_op jit(solution)/shard_map/all_gather | solution.py:170
  379.7 5.0 %select_add_fusion.gram_ref = f32[1024,1024]{1,0:T(8,128)} fusion(f32[1024,1024]{1,0:T(8,128)} %all-gather.5.cloned.1.call-done), kind=kLoop, calls=%fused_computation | loop fusion | flops 4194304 | bytes 8388608 | tf_op jit(solution)/shard_map/add | solution.py:171
  384.7 0.0 all-to-all-done
  384.7 0.0 copy-start.1
  384.8 2.2 copy-done.1
  386.9 51.8 %shard_map.50 = (f32[1024,128]{1,0:T(8,128)}, f32[1,128]{1,0:T(1,128)}) custom-call(f32[1024,1024]{1,0:T(8,128)S(1)} %copy-done.1, f32[1024,128]{1,0:T(8,128)S(1)} %bitcast.13), custom_call_target="tpu_custom_call" | custom-call | tf_op jit(solution)/shard_map/pallas_call | solution.py:120
Async XLA Ops:
  7.2 1.2 copy-start
  7.2 55.1 %all-gather.3.cloned.1.call-start = ((), (), s32[]{:S(2)}) async-start(), calls=%async_computation.1 | async-start | bytes 4718592 | tf_op jit(solution)/shard_map/all_gather | solution.py:163
  12.7 316.1 %copy-start.2 = (f32[1024,128]{1,0:T(8,128)S(1)}, f32[1024,128]{1,0:T(8,128)}, u32[]{:S(2)}) copy-start(f32[1024,128]{1,0:T(8,128)} %fusion.1) | copy-start | bytes 1572868
  12.7 316.1 %all-reduce.2.cloned.1.call-start = ((), (), s32[]{:S(2)}) async-start(), calls=%async_computation.2 | async-start | bytes 1048576 | tf_op jit(solution)/shard_map/psum | solution.py:169
  72.1 307.6 %all-gather.5.cloned.1.call-start = ((), (), s32[]{:S(2)}) async-start(), calls=%async_computation.3 | async-start | bytes 4718592 | tf_op jit(solution)/shard_map/all_gather | solution.py:170
  329.8 54.9 %all-to-all-start = ((f32[8,128,128]{1,2,0:T(8,128)}), f32[8,128,128]{1,2,0:T(8,128)S(1)}, u32[]{:S(2)}, u32[]{:S(2)}) async-start(f32[8,128,128]{1,2,0:T(8,128)} %copy.5), calls=%async_computation | async-start | bytes 1048576 | tf_op jit(solution)/shard_map/all_to_all | solution.py:168
  384.7 2.2 copy-start.1
Sparse Core Ops, SparseCore 0:
  12.8 49.4 all-gather.2
  72.2 256.5 all-reduce.1
  331.1 48.5 all-gather.4

commit v2 on v1

--- a/solution.py
+++ b/solution.py
@@ -1,3 +1,4 @@
+import functools
 import math
 
 import jax
@@ -8,8 +9,6 @@
 from jax.sharding import PartitionSpec as P
 
 ridge_level = 0.1
-
-
 HI = lax.Precision.HIGHEST
 
 
@@ -71,51 +70,58 @@
                 work[first + 8 * i : first + 8 * i + 8, 128 * c : 128 * c + 128] = tiles[i][c]
 
 
-def factor_kernel(gram_ref, rows_ref, factor_ref, score_ref, a_ref, work):
-    total = gram_ref.shape[0]
-    blocks = total // 128
-    a_ref[:, 0:total] = gram_ref[...]
+def factor_kernel(blocks_ref, rows_ref, factor_ref, score_ref, a_ref, work):
+    total = rows_ref.shape[0]
+    count = total // 128
+    total_rows = 128 * lax.axis_size("dp") * lax.axis_size("feat")
+    for f in range(count):
+        for d in range(count // 2):
+            a, b = sorted((f, (f + d) % count))
+            a_ref[128 * a : 128 * a + 128, 128 * b : 128 * b + 128] = (
+                blocks_ref[f, 128 * d : 128 * d + 128, :] * (1.0 / total_rows)
+            )
+        half = 64 * (f // (count // 2))
+        a, b = sorted((f, (f + count // 2) % count))
+        a_ref[128 * a + half : 128 * a + half + 64, 128 * b : 128 * b + 128] = (
+            blocks_ref[f, 128 * (count // 2) : 128 * (count // 2) + 64, :] * (1.0 / total_rows)
+        )
     a_ref[:, total : total + 128] = rows_ref[...]
     eye = (
         lax.broadcasted_iota(jnp.int32, (128, 128), 0)
         == lax.broadcasted_iota(jnp.int32, (128, 128), 1)
     ).astype(jnp.float32)
 
-    @pl.loop(0, blocks)
-    def _(p):
-        r = pl.multiple_of(p * 128, 128)
-        work[:, 0:128] = a_ref[pl.ds(r, 128), pl.ds(r, 128)]
+    for p in range(count):
+        r = 128 * p
+        work[:, 0:128] = a_ref[r : r + 128, r : r + 128] + ridge_level * eye
         work[:, 128:256] = eye
         factor_diagonal(work, 32)
-        a_ref[pl.ds(r, 128), :] = jnp.dot(
+        a_ref[r : r + 128, r + 128 :] = jnp.dot(
             work[:, 128:256],
-            a_ref[pl.ds(r, 128), :],
+            a_ref[r : r + 128, r + 128 :],
             precision=HI,
             preferred_element_type=jnp.float32,
         )
-
-        @pl.loop(p + 1, blocks)
-        def _(i):
-            ri = pl.multiple_of(i * 128, 128)
-            a_ref[pl.ds(ri, 128), :] -= gram_of(
-                a_ref[pl.ds(r, 128), pl.ds(ri, 128)], a_ref[pl.ds(r, 128), :]
+        a_ref[r : r + 128, r : r + 128] = work[:, 0:128]
+        for i in range(p + 1, count):
+            q = 128 * i
+            a_ref[q : q + 128, q:] -= gram_of(
+                a_ref[r : r + 128, q : q + 128], a_ref[r : r + 128, q:]
             )
-
-        a_ref[pl.ds(r, 128), pl.ds(r, 128)] = work[:, 0:128]
 
     solved = a_ref[:, total : total + 128]
     score_ref[...] = jnp.sum(solved * solved, axis=0, keepdims=True) / total
     place = lax.axis_index("feat")
     mine = pl.multiple_of(place * 128, 128)
-    for b in range(blocks):
+    for b in range(count):
         piece = a_ref[pl.ds(mine, 128), 128 * b : 128 * b + 128].T
         below = 128 * b + lax.broadcasted_iota(jnp.int32, (128, 128), 0)
         across = mine + lax.broadcasted_iota(jnp.int32, (128, 128), 1)
         factor_ref[128 * b : 128 * b + 128, :] = jnp.where(below >= across, piece, 0.0)
 
 
-def factor_and_score(gram_full, rows):
-    total = gram_full.shape[0]
+def factor_and_score(blocks, rows):
+    total = rows.shape[0]
     in_vmem = pl.BlockSpec(memory_space=pltpu.VMEM)
     return pl.pallas_call(
         factor_kernel,
@@ -130,46 +136,252 @@
             pltpu.VMEM((128, 256), jnp.float32),
         ],
         compiler_params=pltpu.CompilerParams(vmem_limit_bytes=48 * 2**20),
-    )(gram_full, rows)
-
-
-def halton_phase(halton_start, columns):
-    index_value = halton_start[0] + columns
-    radical = jnp.zeros(columns.shape, jnp.float32)
+    )(blocks, rows)
+
+
+def halton_phase(index_value):
+    radical = jnp.zeros(index_value.shape, jnp.float32)
     for place in range(16):
-        digit_bit = index_value // (1 << place) % 2
+        digit_bit = (index_value >> place) & 1
         radical = radical + digit_bit.astype(jnp.float32) * 0.5 ** (place + 1)
     return 2.0 * math.pi * radical
 
 
-def featurize(row_block, frequencies, phase):
-    angles = jnp.dot(
-        row_block, frequencies, precision=lax.Precision.HIGHEST, preferred_element_type=jnp.float32
-    )
-    return math.sqrt(2.0) * jnp.cos(angles + phase)
+TURN_HIGH = 6.28125
+TURN_LOW = 2.0 * math.pi - TURN_HIGH
+COSINE = (
+    1.4142135623717025,
+    -0.7071067811637958,
+    0.058925565037607174,
+    -0.0019641854397455995,
+    3.507470808988151e-05,
+    -3.897096847328774e-07,
+    2.950756124473042e-09,
+    -1.6054447590940767e-11,
+    5.837442578648932e-14,
+)
+
+
+def scaled_cosine(angle):
+    turns = jnp.floor(angle * (0.5 / math.pi) + 0.5)
+    rest = (angle - turns * TURN_HIGH) - turns * TURN_LOW
+    square = rest * rest
+    value = jnp.full(angle.shape, COSINE[-1], jnp.float32)
+    for coefficient in COSINE[-2::-1]:
+        value = value * square + coefficient
+    return value
+
+
+def gram_kernel(
+    nz, points, own_freq, start, blocks, rows_out,
+    freqs, feats, part, got_y, sum_y, got_z, all_z,
+    fs, fr, ys, yr, zs, zr, gs, gr, hs, hr, xs, xr,
+):
+    dp, f = lax.axis_index("dp"), lax.axis_index("feat")
+    ny, nx, nf = 4, 4, 8
+    z, y, x, core = dp // ny, dp % ny, f // 2, f % 2
+    sibling = (dp, f + 1 - 2 * core)
+    x_peer = [(dp, ((x + k) % nx) * 2 + core) for k in range(nx)]
+    y_peer = [(z * ny + (y + k) % ny, f) for k in range(ny)]
+    z_peer = [(((z + k) % nz) * ny + y, f) for k in range(nz)]
+
+    def send(src, dst, ssem, rsem, to):
+        return pltpu.make_async_remote_copy(
+            src_ref=src, dst_ref=dst, send_sem=ssem, recv_sem=rsem,
+            device_id=to, device_id_type=pl.DeviceIdType.MESH,
+        )
+
+    barrier = pltpu.get_barrier_semaphore()
+    peers = [sibling] + x_peer[1:] + y_peer[1:] + z_peer[1:]
+    for peer in peers:
+        pl.semaphore_signal(barrier, inc=1, device_id=peer, device_id_type=pl.DeviceIdType.MESH)
+    freqs[f] = own_freq[...]
+    pl.semaphore_wait(barrier, len(peers))
+
+    pending = []
+    for k in range(1, nx):
+        copy = send(own_freq, freqs.at[f], fs.at[k], fr.at[f], x_peer[k])
+        copy.start()
+        pending.append(copy)
+    copy = send(own_freq, freqs.at[f], fs.at[0], fr.at[f], sibling)
+    copy.start()
+    pending.append(copy)
+
+    def featurize(g):
+        phase = halton_phase(
+            start[0] + g * 128 + lax.broadcasted_iota(jnp.int32, (1, 128), 1)
+        )
+
+        @pl.loop(0, points.shape[0] // 256)
+        def _(step):
+            rows = pl.ds(pl.multiple_of(step * 256, 256), 256)
+            angle = jnp.dot(
+                points[rows, :], freqs[g], precision=HI, preferred_element_type=jnp.float32
+            )
+            feats[g, rows, :] = scaled_cosine(angle + phase)
+
+    def arrival(g):
+        return send(own_freq, freqs.at[g], fs.at[0], fr.at[g], sibling)
+
+    featurize(f)
+    part[0:128, :] = gram_of(feats[f], feats[f])
+    for k in range(1, nx):
+        g = x_peer[k][1]
+        arrival(g).wait_recv()
+        copy = send(freqs.at[g], freqs.at[g], fs.at[nx + k - 1], fr.at[g], sibling)
+        copy.start()
+        pending.append(copy)
+    other = 1 - core
+    arrival(f + 1 - 2 * core).wait_recv()
+    for k in range(1, nx):
+        arrival(((x + k) % nx) * 2 + other).wait_recv()
+    for d in range(1, nf // 2 + 1):
+        g = (f + d) % nf
+        featurize(g)
+        low, high = jnp.minimum(f, g), jnp.maximum(f, g)
+        if d < nf // 2:
+            part[128 * d : 128 * d + 128, :] = gram_of(feats[low], feats[high])
+        else:
+            sum_y[0:128, :] = gram_of(feats[low], feats[high])
+            half = pl.multiple_of(64 * (f // (nf // 2)), 64)
+            part[128 * d : 128 * d + 64, :] = sum_y[pl.ds(half, 64), :]
+
+    share = part.shape[0] // ny
+    for k in range(1, ny):
+        to = y_peer[k]
+        theirs = pl.ds(pl.multiple_of(((y + k) % ny) * share, 8), share)
+        copy = send(part.at[theirs], got_y.at[k], ys.at[k], yr.at[k], to)
+        copy.start()
+        pending.append(copy)
+
+    own_points = points[pl.ds(pl.multiple_of(f * 128, 128), 128), :]
+    for g in range(nf):
+        angle = lax.dot_general(
+            freqs[g], own_points, (((0,), (1,)), ((), ())),
+            precision=HI, preferred_element_type=jnp.float32,
+        )
+        phase = halton_phase(
+            start[0] + g * 128 + lax.broadcasted_iota(jnp.int32, (128, 128), 0)
+        )
+        rows_out[128 * g : 128 * g + 128, :] = scaled_cosine(angle + phase)
+
+    for copy in pending[-(ny - 1):]:
+        copy.wait_recv()
+    mine = pl.ds(pl.multiple_of(y * share, 8), share)
+    sum_y[...] = ((part[mine, :] + got_y[1]) + got_y[2]) + got_y[3]
+
+    slab = 16
+    owners = share // slab
+    for k in range(1, nz):
+        there = (z + k) % nz
+        back = (z - k + nz) % nz
+
+        @pl.when(there < owners)
+        def _():
+            at = pl.ds(pl.multiple_of(there * slab, slab), slab)
+            send(sum_y.at[at], got_z.at[k], zs.at[k], zr.at[k], z_peer[k]).start()
+
+    @pl.when(z < owners)
+    def _():
+        at = pl.ds(pl.multiple_of(z * slab, slab), slab)
+        total = sum_y[at, :]
+        for k in range(1, nz):
+            send(sum_y.at[0:slab], got_z.at[k], zs.at[k], zr.at[k], z_peer[k]).wait_recv()
+            total = total + got_z[k]
+        all_z[at, :] = total
+        for k in range(1, nz):
+            send(all_z.at[at], all_z.at[at], gs.at[k], gr.at[k], z_peer[k]).start()
+
+    for k in range(1, nz):
+        there = (z + k) % nz
+        back = (z - k + nz) % nz
+
+        @pl.when(there < owners)
+        def _():
+            send(sum_y.at[0:slab], got_z.at[k], zs.at[k], zr.at[k], z_peer[k]).wait_send()
+
+        @pl.when(back < owners)
+        def _():
+            at = pl.ds(pl.multiple_of(back * slab, slab), slab)
+            send(all_z.at[at], all_z.at[at], gs.at[k], gr.at[k], z_peer[k]).wait_recv()
+
+    blocks[f, mine, :] = all_z[...]
+    wide = []
+    for k in range(1, ny):
+        copy = send(all_z, blocks.at[f, mine], hs.at[k], hr.at[k], y_peer[k])
+        copy.start()
+        wide.append(copy)
+    for k in range(1, ny):
+        back = pl.ds(pl.multiple_of(((y - k + ny) % ny) * share, 8), share)
+        send(all_z, blocks.at[f, back], hs.at[k], hr.at[k], y_peer[k]).wait_recv()
+
+    for k in range(1, nx):
+        copy = send(blocks.at[f], blocks.at[f], xs.at[k], xr.at[f], x_peer[k])
+        copy.start()
+        wide.append(copy)
+    copy = send(blocks.at[f], blocks.at[f], xs.at[0], xr.at[f], sibling)
+    copy.start()
+    wide.append(copy)
+
+    def block_arrival(g):
+        return send(blocks.at[g], blocks.at[g], xs.at[0], xr.at[g], sibling)
+
+    for k in range(1, nx):
+        g = x_peer[k][1]
+        block_arrival(g).wait_recv()
+        copy = send(blocks.at[g], blocks.at[g], xs.at[nx + k - 1], xr.at[g], sibling)
+        copy.start()
+        wide.append(copy)
+    block_arrival(f + 1 - 2 * core).wait_recv()
+    for k in range(1, nx):
+        block_arrival(((x + k) % nx) * 2 + other).wait_recv()
+
+    for copy in pending + wide:
+        copy.wait_send()
+
+    @pl.when(z < owners)
+    def _():
+        at = pl.ds(pl.multiple_of(z * slab, slab), slab)
+        for k in range(1, nz):
+            send(all_z.at[at], all_z.at[at], gs.at[k], gr.at[k], z_peer[k]).wait_send()
+
+
+def gram_blocks(points, frequencies, halton_start):
+    nf = lax.axis_size("feat")
+    nz = lax.axis_size("dp") // 4
+    rows, dim = points.shape
+    in_vmem = pl.BlockSpec(memory_space=pltpu.VMEM)
+    length = 128 * (nf // 2) + 64
+    dma = pltpu.SemaphoreType.DMA
+    f32 = jnp.float32
+    return pl.pallas_call(
+        functools.partial(gram_kernel, nz),
+        out_shape=(
+            jax.ShapeDtypeStruct((nf, length, 128), f32),
+            jax.ShapeDtypeStruct((128 * nf, 128), f32),
+        ),
+        in_specs=[in_vmem, in_vmem, pl.BlockSpec(memory_space=pltpu.SMEM)],
+        out_specs=(in_vmem,) * 2,
+        scratch_shapes=[
+            pltpu.VMEM((nf, dim, 128), f32),
+            pltpu.VMEM((nf, rows, 128), f32),
+            pltpu.VMEM((length, 128), f32),
+            pltpu.VMEM((4, length // 4, 128), f32),
+            pltpu.VMEM((length // 4, 128), f32),
+            pltpu.VMEM((nz, 16, 128), f32),
+            pltpu.VMEM((length // 4, 128), f32),
+            dma((8,)), dma((nf,)), dma((4,)), dma((4,)), dma((nz,)), dma((nz,)),
+            dma((nz,)), dma((nz,)), dma((4,)), dma((4,)), dma((8,)), dma((nf,)),
+        ],
+        compiler_params=pltpu.CompilerParams(
+            vmem_limit_bytes=48 * 2**20, collective_id=0, has_side_effects=True
+        ),
+    )(points, frequencies, halton_start)
 
 
 def per_device(points, frequencies, halton_start):
-    panel_width = frequencies.shape[1]
-    feat_count = lax.axis_size("feat")
-    group_count = lax.axis_size("dp")
-    feat_total = panel_width * feat_count
-    row_count = points.shape[0]
-    total_rows = row_count * group_count
-    feat_place = lax.axis_index("feat")
-    columns = feat_place * panel_width + jnp.arange(panel_width, dtype=jnp.int32)
-    own_panel = featurize(points, frequencies, halton_phase(halton_start, columns))
-    gram_block = jnp.dot(
-        lax.all_gather(own_panel, "feat", axis=1, tiled=True).T,
-        own_panel,
-        precision=lax.Precision.HIGHEST,
-        preferred_element_type=jnp.float32,
-    )
-    own_rows = lax.all_to_all(own_panel, "feat", split_axis=0, concat_axis=1, tiled=True)
-    summed = lax.psum(gram_block, "dp")
-    gram_total = lax.all_gather(summed, "feat", axis=1, tiled=True)
-    gram_full = gram_total / total_rows + ridge_level * jnp.eye(feat_total, dtype=jnp.float32)
-    own_factor, scores = factor_and_score(gram_full, own_rows.T)
+    blocks, rows = gram_blocks(points, frequencies, halton_start)
+    own_factor, scores = factor_and_score(blocks, rows)
     return (scores.reshape(128), own_factor)
 
 

time: 446 us -> 123 us (0.28)
  waiting for transfers between devices: 341 us -> 0 us
  Pallas kernels: 51.8 us -> 120 us
  starting transfers between devices: 15.1 us -> 0 us
  matrix products: 14 us -> 0 us
  between operations: 14.5 us -> 1.29 us
  other arithmetic: 5.08 us -> 0 us
    psum x1 -> x0, waiting for transfers between devices: 257 us -> none  [per_device(): summed = lax.psum(gram_block, 'dp')]
    all_gather x2 -> x0, waiting for transfers between devices: 84.5 us -> none  [the longest x1 49.5 us: per_device(): lax.all_gather(own_panel, 'feat', axis=1, tiled=True)]
    pallas_call x0 -> x1, Pallas kernels: none -> 84.2 us  [gram_blocks(): pl.pallas_call(functools.partial(gram_kernel, nz), out_shape=(jax.ShapeDt...]
    pallas_call x1, Pallas kernels: 51.8 us -> 35.6 us  [factor_and_score(): pl.pallas_call(factor_kernel, out_shape=(jax.ShapeDtypeStruct((total, 128...]
    all_to_all x1 -> x0, starting transfers between devices: 15 us -> none  [per_device(): lax.all_to_all(own_panel, 'feat', split_axis=0, concat_axis=1, tiled=True)]
    dot_general x2 -> x0, matrix products: 14 us -> none  [the longest x1 9.76 us: per_device(): jnp.dot(lax.all_gather(own_panel, 'feat', axis=1, tiled=True).T, own_pane...]
    add x1 -> x0, other arithmetic: 5.01 us -> none  [per_device(): gram_total / total_rows]
  transfers between devices with their start and end apart: 4 -> 0, of which waited for: 3 -> 0; matrix products, arithmetic and copies ran while one was open for 1% -> 0% of each run, Pallas kernels for 0% -> 0%
where the time goes in v2:
time: 123 us
  Pallas kernels  120 us (98%)
  local copies, waits for them, and re-layouts  2.12 us (2%)
  between operations  1.29 us (1%)
    pallas_call x1, Pallas kernels, gram_blocks(): pl.pallas_call(functools.partial(gram_kernel, nz), out_shape=(jax.ShapeDt...  84.2 us
    pallas_call x1, Pallas kernels, factor_and_score(): pl.pallas_call(factor_kernel, out_shape=(jax.ShapeDtypeStruct((total, 128...  35.6 us

profile of v2, /device:TPU:1, one launch (start us, length us, event | category | flops | bytes accessed | tf_op | source)
XLA Modules:
  0.0 123.2 jit_solution(12872780114951085162)
XLA Ops:
  1.3 0.0 copy-start
  1.3 1.2 copy-done
  2.5 0.0 copy-start.1
  2.5 0.9 copy-done.1
  3.4 84.2 %shard_map.50 = (f32[8,576,128]{2,1,0:T(8,128)S(1)}, f32[1024,128]{1,0:T(8,128)S(1)}) custom-call(f32[1024,256]{1,0:T(8,128)S(1)} %copy-done, f32[256,128]{1,0:T(8,128)S(1)} %copy-done.1, s32[1]{0:T(128)S(6)} %copy.5.start), custom_call_target="tpu_custom_call" | custom-call | tf_op jit(solution)/shard_map/pallas_call | solution.py:357
  87.6 35.6 %shard_map.51 = (f32[1024,128]{1,0:T(8,128)}, f32[1,128]{1,0:T(1,128)}) custom-call(f32[8,576,128]{2,1,0:T(8,128)S(1)} %get-tuple-element.6.blocks_ref, f32[1024,128]{1,0:T(8,128)S(1)} %get-tuple-element.7.rows_ref), custom_call_target="tpu_custom_call" | custom-call | tf_op jit(solution)/shard_map/pallas_call | solution.py:126
Async XLA Ops:
  1.3 1.2 copy-start
  2.5 0.9 copy-start.1

commit v3 on v2

v3 whole, which is shorter than its diff:
```python
import functools
import math

import jax
import jax.numpy as jnp
from jax import lax
from jax.experimental import pallas as pl
from jax.experimental.pallas import tpu as pltpu
from jax.sharding import PartitionSpec as P

ridge_level = 0.1
HI = lax.Precision.HIGHEST


def spread_row(tile, place):
    return jnp.broadcast_to(tile[place : place + 1, :], (8, 128))


def gram_of(left, right):
    return lax.dot_general(
        left, right, (((0,), (0,)), ((), ())), precision=HI, preferred_element_type=jnp.float32
    )


def eliminate(tiles, first, width):
    row = lax.broadcasted_iota(jnp.int32, (8, 128), 0)
    depth = width // 8
    column = [[None] * depth for _ in range(width)]
    for k in range(width):
        for i in range(k // 8, depth):
            column[k][i] = jnp.broadcast_to(tiles[i][0][:, first + k : first + k + 1], (8, 128))
    pivots = [jnp.ones((8, 128), jnp.float32) for _ in range(depth)]
    for k in range(width):
        kt, ks = k // 8, k % 8
        pivot = spread_row(column[k][kt], ks)
        pivots[kt] = jnp.where(row == ks, pivot, pivots[kt])
        if k == width - 1:
            break
        inverse = 1.0 / pivot
        weight = {i: column[k][i] * inverse for i in range(kt, depth)}
        weight[kt] = jnp.where(row > ks, weight[kt], 0.0)
        for m in range(k + 1, width):
            x = spread_row(column[k][m // 8], m % 8)
            for i in range(m // 8, depth):
                column[m][i] = column[m][i] - weight[i] * x
        for c in range(len(tiles[0])):
            t = spread_row(tiles[kt][c], ks)
            for i in range(kt + (ks == 7), depth):
                tiles[i][c] = tiles[i][c] - weight[i] * t
    for i in range(depth):
        scale = lax.rsqrt(pivots[i])
        tiles[i] = [t * scale for t in tiles[i]]
    return tiles


def factor_diagonal(work, width):
    for s in range(128 // width):
        first = s * width
        block = work[first : first + width, :]
        if s:
            above = work[0:first, :]
            block = block - gram_of(above[:, first : first + width], above)
        tiles = [
            [block[8 * i : 8 * i + 8, 128 * c : 128 * c + 128] for c in range(2)]
            for i in range(width // 8)
        ]
        tiles = eliminate(tiles, first, width)
        for i in range(width // 8):
            for c in range(2):
                work[first + 8 * i : first + 8 * i + 8, 128 * c : 128 * c + 128] = tiles[i][c]


def halton_phase(index_value):
    radical = jnp.zeros(index_value.shape, jnp.float32)
    for place in range(16):
        digit_bit = (index_value >> place) & 1
        radical = radical + digit_bit.astype(jnp.float32) * 0.5 ** (place + 1)
    return 2.0 * math.pi * radical


TURN_HIGH = 6.28125
TURN_LOW = 2.0 * math.pi - TURN_HIGH
COSINE = (
    1.4142135623717025,
    -0.7071067811637958,
    0.058925565037607174,
    -0.0019641854397455995,
    3.507470808988151e-05,
    -3.897096847328774e-07,
    2.950756124473042e-09,
    -1.6054447590940767e-11,
    5.837442578648932e-14,
)


def scaled_cosine(angle):
    turns = jnp.floor(angle * (0.5 / math.pi) + 0.5)
    rest = (angle - turns * TURN_HIGH) - turns * TURN_LOW
    square = rest * rest
    value = jnp.full(angle.shape, COSINE[-1], jnp.float32)
    for coefficient in COSINE[-2::-1]:
        value = value * square + coefficient
    return value


def leverage_kernel(
    nz, points, own_freq, start, factor_ref, score_ref,
    freqs, feats, block, part, got_y, sum_y, got_z, all_z, blocks, a_ref, work, inverses,
    fs, fr, ys, yr, zs, zr, gs, gr, hs, hr, xs, xr,
):
    dp, f = lax.axis_index("dp"), lax.axis_index("feat")
    ny, nx, nf = 4, 4, 8
    half_way = nf // 2
    total = 128 * nf
    total_rows = points.shape[0] * nz * ny
    z, y, x, core = dp // ny, dp % ny, f // 2, f % 2
    other = 1 - core
    near = f + 1 - 2 * core
    sibling = (dp, near)
    x_peer = [(dp, ((x + k) % nx) * 2 + core) for k in range(nx)]
    y_peer = [(z * ny + (y + k) % ny, f) for k in range(ny)]
    z_peer = [(((z + k) % nz) * ny + y, f) for k in range(nz)]
    sent = []

    def send(src, dst, ssem, rsem, to):
        return pltpu.make_async_remote_copy(
            src_ref=src, dst_ref=dst, send_sem=ssem, recv_sem=rsem,
            device_id=to, device_id_type=pl.DeviceIdType.MESH,
        )

    def go(src, dst, ssem, rsem, to):
        copy = send(src, dst, ssem, rsem, to)
        copy.start()
        sent.append(copy)
        return copy

    barrier = pltpu.get_barrier_semaphore()
    peers = [sibling] + x_peer[1:] + y_peer[1:] + z_peer[1:]
    for peer in peers:
        pl.semaphore_signal(barrier, inc=1, device_id=peer, device_id_type=pl.DeviceIdType.MESH)

    def featurize(g):
        phase = halton_phase(
            start[0] + g * 128 + lax.broadcasted_iota(jnp.int32, (1, 128), 1)
        )

        @pl.loop(0, points.shape[0] // 256)
        def _(step):
            rows = pl.ds(pl.multiple_of(step * 256, 256), 256)
            angle = jnp.dot(
                points[rows, :], freqs[g], precision=HI, preferred_element_type=jnp.float32
            )
            feats[g, rows, :] = scaled_cosine(angle + phase)

    def pair(g):
        featurize(g)
        low, high = jnp.minimum(f, g), jnp.maximum(f, g)
        block[...] = gram_of(feats[low], feats[high])

    def keep(d):
        at = pl.ds(32 * d if isinstance(d, int) else pl.multiple_of(32 * d, 32), 32)
        for q in range(ny):
            part[q, at, :] = block[32 * q : 32 * q + 32, :]

    def keep_half():
        half = 64 * (f // half_way)
        for q in range(ny):
            rows = pl.ds(pl.multiple_of(half + 16 * q, 16), 16)
            part[q, 32 * half_way : 32 * half_way + 16, :] = block[rows, :]

    def panel_in(g):
        send(own_freq, freqs.at[g], fs.at[0], fr.at[g], sibling).wait_recv()

    def pass_panel(k):
        g = x_peer[k][1]
        panel_in(g)
        go(freqs.at[g], freqs.at[g], fs.at[nx + k - 1], fr.at[g], sibling)
        return g

    freqs[f] = own_freq[...]
    pair(f)
    keep(0)
    pl.semaphore_wait(barrier, len(peers))
    go(own_freq, freqs.at[f], fs.at[0], fr.at[f], sibling)
    for k in (3, 2, 1):
        go(own_freq, freqs.at[f], fs.at[k], fr.at[f], x_peer[k])

    panel_in(near)

    @pl.when(core == 0)
    def _():
        pair(near)
        keep(1)

    g = pass_panel(1)
    pair(g)
    keep(2)
    second = pass_panel(2)
    g = ((x + 1) % nx) * 2 + other
    panel_in(g)
    pair(g)
    keep((g - f + nf) % nf)
    pair(second)
    keep_half()
    last = ((x + 2) % nx) * 2 + other
    panel_in(last)

    @pl.when(core == 1)
    def _():
        pair(last)
        keep(3)

    share = part.shape[1]
    to_y = []
    for k in range(1, ny):
        to_y.append(go(part.at[(y + k) % ny], got_y.at[k], ys.at[k], yr.at[k], y_peer[k]))

    pass_panel(3)
    panel_in(((x + 3) % nx) * 2 + other)
    own_points = points[pl.ds(pl.multiple_of(f * 128, 128), 128), :]
    for g in range(nf):
        angle = lax.dot_general(
            freqs[g], own_points, (((0,), (1,)), ((), ())),
            precision=HI, preferred_element_type=jnp.float32,
        )
        phase = halton_phase(
            start[0] + g * 128 + lax.broadcasted_iota(jnp.int32, (128, 128), 0)
        )
        a_ref[128 * g : 128 * g + 128, total : total + 128] = scaled_cosine(angle + phase)

    for copy in to_y:
        copy.wait_recv()
    sum_y[...] = ((part[y] + got_y[1]) + got_y[2]) + got_y[3]

    slab = 16
    owners = share // slab
    for k in range(1, nz):
        there = (z + k) % nz

        @pl.when(there < owners)
        def _():
            at = pl.ds(pl.multiple_of(there * slab, slab), slab)
            send(sum_y.at[at], got_z.at[k], zs.at[k], zr.at[k], z_peer[k]).start()

    own_slab = pl.ds(pl.multiple_of(jnp.minimum(z, owners - 1) * slab, slab), slab)

    @pl.when(z < owners)
    def _():
        whole = sum_y[own_slab, :]
        for k in range(1, nz):
            send(sum_y.at[0:slab], got_z.at[k], zs.at[k], zr.at[k], z_peer[k]).wait_recv()
            whole = whole + got_z[k]
        all_z[own_slab, :] = whole
        for k in range(1, nz):
            send(all_z.at[own_slab], all_z.at[own_slab], gs.at[k], gr.at[z], z_peer[k]).start()

    def rows_of(d):
        return 32 if d < half_way else 16

    for d in range(half_way + 1):
        for owner in range(2 * d, min(2 * d + 2, owners)):

            @pl.when(z != owner)
            def _():
                at = slice(owner * slab, owner * slab + slab)
                send(all_z.at[at], all_z.at[at], gs.at[1], gr.at[owner], z_peer[1]).wait_recv()

        n = rows_of(d)
        mine = pl.ds(pl.multiple_of(128 * d + n * y, 16), n)
        blocks[f, mine, :] = all_z[32 * d : 32 * d + n, :]
        for k in range(1, ny):
            go(all_z.at[32 * d : 32 * d + n], blocks.at[f, mine], hs.at[k, d], hr.at[k, d], y_peer[k])

    for d in range(half_way + 1):
        n = rows_of(d)
        for k in range(1, ny):
            back = pl.ds(pl.multiple_of(128 * d + n * ((y - k + ny) % ny), 16), n)
            send(
                all_z.at[32 * d : 32 * d + n], blocks.at[f, back], hs.at[k, d], hr.at[k, d], y_peer[k]
            ).wait_recv()
        piece = blocks.at[f, 128 * d : 128 * d + 4 * n]
        go(piece, piece, xs.at[0, d], xr.at[f * 5 + d], sibling)
        for k in (3, 2, 1):
            go(piece, piece, xs.at[k, d], xr.at[f * 5 + d], x_peer[k])

    def piece_in(g, d):
        piece = blocks.at[g, 128 * d : 128 * d + 4 * rows_of(d)]
        send(piece, piece, xs.at[0, d], xr.at[g * 5 + d], sibling).wait_recv()
        return piece

    def round_in(d):
        for k in (1, 3, 2):
            g = x_peer[k][1]
            piece = piece_in(g, d)
            send(piece, piece, xs.at[nx + k - 1, d], xr.at[g * 5 + d], sibling).start()
        piece_in(near, d)
        for k in (1, 3, 2):
            piece_in(((x + k) % nx) * 2 + other, d)

    eye = (
        lax.broadcasted_iota(jnp.int32, (128, 128), 0)
        == lax.broadcasted_iota(jnp.int32, (128, 128), 1)
    ).astype(jnp.float32)

    def load(a, b):
        scale = 1.0 / total_rows
        apart = b - a
        r, c = 128 * a, 128 * b
        if apart == half_way:
            top = 128 * half_way
            a_ref[r : r + 64, c : c + 128] = blocks[a, top : top + 64, :] * scale
            a_ref[r + 64 : r + 128, c : c + 128] = blocks[b, top : top + 64, :] * scale
            return
        owner, d = (a, apart) if apart < half_way else (b, nf - apart)
        value = blocks[owner, 128 * d : 128 * d + 128, :] * scale
        a_ref[r : r + 128, c : c + 128] = value + ridge_level * eye if a == b else value

    def advance(m, left, right):
        r = 128 * m
        a_ref[r : r + 128, 128 * left : 128 * right] = jnp.dot(
            inverses[m], a_ref[r : r + 128, 128 * left : 128 * right],
            precision=HI, preferred_element_type=jnp.float32,
        )
        for i in range(m + 1, min(right, nf)):
            q = 128 * i
            span = slice(128 * max(i, left), 128 * right)
            a_ref[q : q + 128, span] -= gram_of(
                a_ref[r : r + 128, q : q + 128], a_ref[r : r + 128, span]
            )

    joins = {0: (1, 2), 1: (2, 4), 2: (4, nf + 1)}
    rounds = {0: (1,), 1: (2, 3), 2: (4,)}

    def begin(p):
        r = 128 * p
        work[:, 0:128] = a_ref[r : r + 128, r : r + 128]
        work[:, 128:256] = eye

    round_in(0)
    load(0, 0)
    begin(0)

    @pl.loop(0, nf)
    def _(p):
        factor_diagonal(work, 32)
        inverses[p] = work[:, 128:256]
        for k in range(nf):

            @pl.when(p == k)
            def _():
                r = 128 * k
                a_ref[r : r + 128, r : r + 128] = work[:, 0:128]
                for d in rounds.get(k, ()):
                    round_in(d)
                if k in joins:
                    left, right = joins[k]
                    for b in range(left, min(right, nf)):
                        for a in range(b + 1):
                            load(a, b)
                    for m in range(k):
                        advance(m, left, right)
                advance(k, k + 1, joins[min(k, 2)][1])
                if k + 1 < nf:
                    begin(k + 1)

    solved = a_ref[:, total : total + 128]
    score_ref[...] = jnp.sum(solved * solved, axis=0, keepdims=True) / total
    mine = pl.multiple_of(f * 128, 128)
    for b in range(nf):
        value = a_ref[pl.ds(mine, 128), 128 * b : 128 * b + 128].T
        below = 128 * b + lax.broadcasted_iota(jnp.int32, (128, 128), 0)
        across = mine + lax.broadcasted_iota(jnp.int32, (128, 128), 1)
        factor_ref[128 * b : 128 * b + 128, :] = jnp.where(below >= across, value, 0.0)

    for copy in sent:
        copy.wait_send()
    for d in range(half_way + 1):
        for k in (1, 3, 2):
            piece = blocks.at[f, 128 * d : 128 * d + 4 * rows_of(d)]
            send(piece, piece, xs.at[nx + k - 1, d], xr.at[f * 5 + d], sibling).wait_send()
    for k in range(1, nz):

        @pl.when((z + k) % nz < owners)
        def _():
            send(sum_y.at[0:slab], got_z.at[k], zs.at[k], zr.at[k], z_peer[k]).wait_send()

    @pl.when(z < owners)
    def _():
        for k in range(1, nz):
            send(all_z.at[own_slab], all_z.at[own_slab], gs.at[k], gr.at[z], z_peer[k]).wait_send()


def per_device(points, frequencies, halton_start):
    nf = lax.axis_size("feat")
    nz = lax.axis_size("dp") // 4
    rows, dim = points.shape
    total = 128 * nf
    in_vmem = pl.BlockSpec(memory_space=pltpu.VMEM)
    share = 16 * nf + 16
    f32 = jnp.float32
    dma = pltpu.SemaphoreType.DMA
    own_factor, scores = pl.pallas_call(
        functools.partial(leverage_kernel, nz),
        out_shape=(
            jax.ShapeDtypeStruct((total, 128), f32),
            jax.ShapeDtypeStruct((1, 128), f32),
        ),
        in_specs=[in_vmem, in_vmem, pl.BlockSpec(memory_space=pltpu.SMEM)],
        out_specs=(in_vmem,) * 2,
        scratch_shapes=[
            pltpu.VMEM((nf, dim, 128), f32),
            pltpu.VMEM((nf, rows, 128), f32),
            pltpu.VMEM((128, 128), f32),
            pltpu.VMEM((4, share, 128), f32),
            pltpu.VMEM((4, share, 128), f32),
            pltpu.VMEM((share, 128), f32),
            pltpu.VMEM((nz, 16, 128), f32),
            pltpu.VMEM((share, 128), f32),
            pltpu.VMEM((nf, 4 * share, 128), f32),
            pltpu.VMEM((total, total + 128), f32),
            pltpu.VMEM((128, 256), f32),
            pltpu.VMEM((nf, 128, 128), f32),
            dma((8,)), dma((nf,)), dma((4,)), dma((4,)), dma((nz,)), dma((nz,)),
            dma((nz,)), dma((nz,)), dma((4, 5)), dma((4, 5)), dma((8, 5)), dma((5 * nf,)),
        ],
        compiler_params=pltpu.CompilerParams(
            vmem_limit_bytes=48 * 2**20, collective_id=0, has_side_effects=True
        ),
    )(points, frequencies, halton_start)
    return (scores.reshape(128), own_factor)


def solution(mesh):
    in_specs = (P("dp", None), P(None, "feat"), P())
    out_specs = (P(("dp", "feat")), P(None, "feat"))
    return jax.shard_map(
        per_device, mesh=mesh, in_specs=in_specs, out_specs=out_specs, check_vma=False
    )
```

time: 123 us -> 114 us (0.927)
  Pallas kernels: 120 us -> 110 us
  local copies, waits for them, and re-layouts: 2.12 us -> 3.43 us
    pallas_call x2 -> x1, Pallas kernels: 120 us -> 110 us  [per_device(): pl.pallas_call(functools.partial(leverage_kernel, nz), out_shape=(jax.Sha...]
    unnamed x4 -> x6, local copies, waits for them, and re-layouts: 2.12 us -> 3.43 us
where the time goes in v3:
time: 114 us
  Pallas kernels  110 us (96%)
  local copies, waits for them, and re-layouts  3.43 us (3%)
  between operations  1.29 us (1%)
    pallas_call x1, Pallas kernels, per_device(): pl.pallas_call(functools.partial(leverage_kernel, nz), out_shape=(jax.Sha...  110 us
    unnamed x6, local copies, waits for them, and re-layouts  3.43 us

profile of v3, /device:TPU:1, one launch (start us, length us, event | category | flops | bytes accessed | tf_op | source)
XLA Modules:
  0.0 114.2 jit_solution(12270038522870860135)
XLA Ops:
  1.3 0.0 copy-start
  1.3 1.2 %copy-done = f32[1024,256]{1,0:T(8,128)S(1)} copy-done((f32[1024,256]{1,0:T(8,128)S(1)}, f32[1024,256]{1,0:T(8,128)}, u32[]{:S(2)}) %copy-start) | copy-done | bytes 1048600
  2.5 0.0 copy-start.1
  2.5 0.9 copy-done.1
  3.4 109.5 %shard_map.50 = (f32[1024,128]{1,0:T(8,128)S(1)}, f32[1,128]{1,0:T(1,128)S(1)}) custom-call(f32[1024,256]{1,0:T(8,128)S(1)} %copy-done, f32[256,128]{1,0:T(8,128)S(1)} %copy-done.1, s32[1]{0:T(128)S(6)} %copy.7.start), custom_call_target="tpu_custom_call" | custom-call | tf_op jit(solution)/shard_map/pallas_call | solution.py:402
  112.9 0.5 copy.8
  113.4 0.8 copy.9
Async XLA Ops:
  1.3 1.2 %copy-start = (f32[1024,256]{1,0:T(8,128)S(1)}, f32[1024,256]{1,0:T(8,128)}, u32[]{:S(2)}) copy-start(f32[1024,256]{1,0:T(8,128)} %points.1) | copy-start | bytes 3145732
  2.5 0.9 copy-start.1

commit v4 on v3

--- a/solution.py
+++ b/solution.py
@@ -162,6 +162,19 @@
         for q in range(ny):
             part[q, at, :] = block[32 * q : 32 * q + 32, :]
 
+    def rows_of(d):
+        return 16 if isinstance(d, int) and d == half_way else 32
+
+    def y_copy(k, d):
+        n = rows_of(d)
+        at = pl.ds(32 * d if isinstance(d, int) else pl.multiple_of(32 * d, 32), n)
+        to = (y + k) % ny
+        return send(part.at[to, at], got_y.at[k, at], ys.at[k * 5 + d], yr.at[k * 5 + d], y_peer[k])
+
+    def pass_on(d):
+        for k in range(1, ny):
+            y_copy(k, d).start()
+
     def keep_half():
         half = 64 * (f // half_way)
         for q in range(ny):
@@ -182,8 +195,9 @@
     keep(0)
     pl.semaphore_wait(barrier, len(peers))
     go(own_freq, freqs.at[f], fs.at[0], fr.at[f], sibling)
-    for k in (3, 2, 1):
+    for k in (3, 2):
         go(own_freq, freqs.at[f], fs.at[k], fr.at[f], x_peer[k])
+    pass_on(0)
 
     panel_in(near)
 
@@ -191,17 +205,21 @@
     def _():
         pair(near)
         keep(1)
+        pass_on(1)
 
     g = pass_panel(1)
     pair(g)
     keep(2)
+    pass_on(2)
     second = pass_panel(2)
     g = ((x + 1) % nx) * 2 + other
     panel_in(g)
     pair(g)
     keep((g - f + nf) % nf)
+    pass_on((g - f + nf) % nf)
     pair(second)
     keep_half()
+    pass_on(half_way)
     last = ((x + 2) % nx) * 2 + other
     panel_in(last)
 
@@ -209,11 +227,30 @@
     def _():
         pair(last)
         keep(3)
+        pass_on(3)
 
     share = part.shape[1]
-    to_y = []
-    for k in range(1, ny):
-        to_y.append(go(part.at[(y + k) % ny], got_y.at[k], ys.at[k], yr.at[k], y_peer[k]))
+    go(own_freq, freqs.at[f], fs.at[1], fr.at[f], x_peer[1])
+    for d in range(half_way + 1):
+        for k in range(1, ny):
+            y_copy(k, d).wait_recv()
+    sum_y[...] = ((part[y] + got_y[1]) + got_y[2]) + got_y[3]
+
+    slab = 16
+    owners = share // slab
+    own_slab = pl.ds(pl.multiple_of(jnp.minimum(z, owners - 1) * slab, slab), slab)
+
+    def to_owner(owner):
+        at = slice(owner * slab, owner * slab + slab)
+        return send(
+            sum_y.at[at], got_z.at[z], zs.at[owner], zr.at[z], (owner * ny + y, f)
+        )
+
+    for owner in range(owners):
+
+        @pl.when(z != owner)
+        def _():
+            to_owner(owner).start()
 
     pass_panel(3)
     panel_in(((x + 3) % nx) * 2 + other)
@@ -228,36 +265,33 @@
         )
         a_ref[128 * g : 128 * g + 128, total : total + 128] = scaled_cosine(angle + phase)
 
-    for copy in to_y:
-        copy.wait_recv()
-    sum_y[...] = ((part[y] + got_y[1]) + got_y[2]) + got_y[3]
-
-    slab = 16
-    owners = share // slab
-    for k in range(1, nz):
-        there = (z + k) % nz
-
-        @pl.when(there < owners)
-        def _():
-            at = pl.ds(pl.multiple_of(there * slab, slab), slab)
-            send(sum_y.at[at], got_z.at[k], zs.at[k], zr.at[k], z_peer[k]).start()
-
-    own_slab = pl.ds(pl.multiple_of(jnp.minimum(z, owners - 1) * slab, slab), slab)
-
     @pl.when(z < owners)
     def _():
-        whole = sum_y[own_slab, :]
-        for k in range(1, nz):
-            send(sum_y.at[0:slab], got_z.at[k], zs.at[k], zr.at[k], z_peer[k]).wait_recv()
-            whole = whole + got_z[k]
+        got_z[z] = sum_y[own_slab, :]
+        for source in range(nz):
+
+            @pl.when(z != source)
+            def _():
+                send(
+                    sum_y.at[0:slab], got_z.at[source], zs.at[0], zr.at[source], z_peer[1]
+                ).wait_recv()
+
+        whole = got_z[0]
+        for source in range(1, nz):
+            whole = whole + got_z[source]
         all_z[own_slab, :] = whole
-        for k in range(1, nz):
+        for k in sorted(range(1, nz), key=lambda k: -min(k, nz - k)):
             send(all_z.at[own_slab], all_z.at[own_slab], gs.at[k], gr.at[z], z_peer[k]).start()
 
-    def rows_of(d):
-        return 32 if d < half_way else 16
-
-    for d in range(half_way + 1):
+    def gather_y(d, k):
+        n = rows_of(d)
+        mine = pl.ds(pl.multiple_of(128 * d + n * y, 16), n)
+        return send(
+            all_z.at[32 * d : 32 * d + n], blocks.at[f, mine],
+            hs.at[k, d], hr.at[k, d], y_peer[k],
+        )
+
+    def spread_y(d):
         for owner in range(2 * d, min(2 * d + 2, owners)):
 
             @pl.when(z != owner)
@@ -269,33 +303,27 @@
         mine = pl.ds(pl.multiple_of(128 * d + n * y, 16), n)
         blocks[f, mine, :] = all_z[32 * d : 32 * d + n, :]
         for k in range(1, ny):
-            go(all_z.at[32 * d : 32 * d + n], blocks.at[f, mine], hs.at[k, d], hr.at[k, d], y_peer[k])
-
-    for d in range(half_way + 1):
-        n = rows_of(d)
+            gather_y(d, k).start()
+
+    def round_copy(g, d, k, to):
+        piece = blocks.at[g, 128 * d : 128 * d + 4 * rows_of(d)]
+        return send(piece, piece, xs.at[k, d], xr.at[g * 5 + d], to)
+
+    def round_out(d):
         for k in range(1, ny):
-            back = pl.ds(pl.multiple_of(128 * d + n * ((y - k + ny) % ny), 16), n)
-            send(
-                all_z.at[32 * d : 32 * d + n], blocks.at[f, back], hs.at[k, d], hr.at[k, d], y_peer[k]
-            ).wait_recv()
-        piece = blocks.at[f, 128 * d : 128 * d + 4 * n]
-        go(piece, piece, xs.at[0, d], xr.at[f * 5 + d], sibling)
+            gather_y(d, k).wait_recv()
+        round_copy(f, d, 0, sibling).start()
         for k in (3, 2, 1):
-            go(piece, piece, xs.at[k, d], xr.at[f * 5 + d], x_peer[k])
-
-    def piece_in(g, d):
-        piece = blocks.at[g, 128 * d : 128 * d + 4 * rows_of(d)]
-        send(piece, piece, xs.at[0, d], xr.at[g * 5 + d], sibling).wait_recv()
-        return piece
+            round_copy(f, d, k, x_peer[k]).start()
 
     def round_in(d):
         for k in (1, 3, 2):
             g = x_peer[k][1]
-            piece = piece_in(g, d)
-            send(piece, piece, xs.at[nx + k - 1, d], xr.at[g * 5 + d], sibling).start()
-        piece_in(near, d)
+            round_copy(g, d, 0, sibling).wait_recv()
+            round_copy(g, d, nx + k - 1, sibling).start()
+        round_copy(near, d, 0, sibling).wait_recv()
         for k in (1, 3, 2):
-            piece_in(((x + k) % nx) * 2 + other, d)
+            round_copy(((x + k) % nx) * 2 + other, d, 0, sibling).wait_recv()
 
     eye = (
         lax.broadcasted_iota(jnp.int32, (128, 128), 0)
@@ -328,17 +356,24 @@
                 a_ref[r : r + 128, q : q + 128], a_ref[r : r + 128, span]
             )
 
-    joins = {0: (1, 2), 1: (2, 4), 2: (4, nf + 1)}
-    rounds = {0: (1,), 1: (2, 3), 2: (4,)}
+    joins = {0: (1, 2), 1: (2, 3), 2: (3, 4), 3: (4, nf + 1)}
 
     def begin(p):
         r = 128 * p
         work[:, 0:128] = a_ref[r : r + 128, r : r + 128]
         work[:, 128:256] = eye
 
+    spread_y(0)
+    round_out(0)
+    for d in range(1, half_way + 1):
+        spread_y(d)
+    for k in (3, 2, 1):
+        round_copy(f, 0, k, x_peer[k]).wait_send()
+    round_out(1)
     round_in(0)
     load(0, 0)
     begin(0)
+    round_out(2)
 
     @pl.loop(0, nf)
     def _(p):
@@ -350,8 +385,10 @@
             def _():
                 r = 128 * k
                 a_ref[r : r + 128, r : r + 128] = work[:, 0:128]
-                for d in rounds.get(k, ()):
-                    round_in(d)
+                if k < half_way:
+                    round_in(k + 1)
+                if k + 3 <= half_way:
+                    round_out(k + 3)
                 if k in joins:
                     left, right = joins[k]
                     for b in range(left, min(right, nf)):
@@ -359,7 +396,7 @@
                             load(a, b)
                     for m in range(k):
                         advance(m, left, right)
-                advance(k, k + 1, joins[min(k, 2)][1])
+                advance(k, k + 1, joins[min(k, 3)][1])
                 if k + 1 < nf:
                     begin(k + 1)
 
@@ -375,14 +412,17 @@
     for copy in sent:
         copy.wait_send()
     for d in range(half_way + 1):
-        for k in (1, 3, 2):
-            piece = blocks.at[f, 128 * d : 128 * d + 4 * rows_of(d)]
-            send(piece, piece, xs.at[nx + k - 1, d], xr.at[f * 5 + d], sibling).wait_send()
-    for k in range(1, nz):
-
-        @pl.when((z + k) % nz < owners)
+        for k in range(1, ny):
+            y_copy(k, d).wait_send()
+            gather_y(d, k).wait_send()
+        for k in range(7):
+            if d > 0 or k not in (1, 2, 3):
+                round_copy(f, d, k, sibling).wait_send()
+    for owner in range(owners):
+
+        @pl.when(z != owner)
         def _():
-            send(sum_y.at[0:slab], got_z.at[k], zs.at[k], zr.at[k], z_peer[k]).wait_send()
+            to_owner(owner).wait_send()
 
     @pl.when(z < owners)
     def _():
@@ -420,7 +460,7 @@
             pltpu.VMEM((total, total + 128), f32),
             pltpu.VMEM((128, 256), f32),
             pltpu.VMEM((nf, 128, 128), f32),
-            dma((8,)), dma((nf,)), dma((4,)), dma((4,)), dma((nz,)), dma((nz,)),
+            dma((8,)), dma((nf,)), dma((20,)), dma((20,)), dma((nz,)), dma((nz,)),
             dma((nz,)), dma((nz,)), dma((4, 5)), dma((4, 5)), dma((8, 5)), dma((5 * nf,)),
         ],
         compiler_params=pltpu.CompilerParams(

time: 114 us -> 110 us (0.965)
  Pallas kernels: 110 us -> 105 us
    pallas_call x1, Pallas kernels: 110 us -> 105 us  [per_device(): pl.pallas_call(functools.partial(leverage_kernel, nz), out_shape=(jax.Sha...]
where the time goes in v4:
time: 110 us; the launch traced here: 109 us
  Pallas kernels  105 us (95%)
  local copies, waits for them, and re-layouts  3.43 us (3%)
  between operations  1.29 us (1%)
    pallas_call x1, Pallas kernels, per_device(): pl.pallas_call(functools.partial(leverage_kernel, nz), out_shape=(jax.Sha...  105 us
    unnamed x6, local copies, waits for them, and re-layouts  3.43 us

profile of v4, /device:TPU:1, one launch (start us, length us, event | category | flops | bytes accessed | tf_op | source)
XLA Modules:
  0.0 109.3 jit_solution(16473220163552094339)
XLA Ops:
  1.3 0.0 copy-start
  1.3 1.2 %copy-done = f32[1024,256]{1,0:T(8,128)S(1)} copy-done((f32[1024,256]{1,0:T(8,128)S(1)}, f32[1024,256]{1,0:T(8,128)}, u32[]{:S(2)}) %copy-start) | copy-done | bytes 1048600
  2.5 0.0 copy-start.1
  2.5 0.9 copy-done.1
  3.4 104.6 %shard_map.50 = (f32[1024,128]{1,0:T(8,128)S(1)}, f32[1,128]{1,0:T(1,128)S(1)}) custom-call(f32[1024,256]{1,0:T(8,128)S(1)} %copy-done, f32[256,128]{1,0:T(8,128)S(1)} %copy-done.1, s32[1]{0:T(128)S(6)} %copy.7.start), custom_call_target="tpu_custom_call" | custom-call | tf_op jit(solution)/shard_map/pallas_call | solution.py:442
  108.0 0.5 copy.8
  108.5 0.8 copy.9
Async XLA Ops:
  1.3 1.2 %copy-start = (f32[1024,256]{1,0:T(8,128)S(1)}, f32[1024,256]{1,0:T(8,128)}, u32[]{:S(2)}) copy-start(f32[1024,256]{1,0:T(8,128)} %points.1) | copy-start | bytes 3145732
  2.5 0.9 copy-start.1

commit v5 on v4

--- a/solution.py
+++ b/solution.py
@@ -22,31 +22,38 @@
     )
 
 
-def eliminate(tiles, first, width):
+def eliminate(tiles, first, width, group=16):
     row = lax.broadcasted_iota(jnp.int32, (8, 128), 0)
     depth = width // 8
-    column = [[None] * depth for _ in range(width)]
-    for k in range(width):
-        for i in range(k // 8, depth):
-            column[k][i] = jnp.broadcast_to(tiles[i][0][:, first + k : first + k + 1], (8, 128))
     pivots = [jnp.ones((8, 128), jnp.float32) for _ in range(depth)]
-    for k in range(width):
-        kt, ks = k // 8, k % 8
-        pivot = spread_row(column[k][kt], ks)
-        pivots[kt] = jnp.where(row == ks, pivot, pivots[kt])
-        if k == width - 1:
-            break
-        inverse = 1.0 / pivot
-        weight = {i: column[k][i] * inverse for i in range(kt, depth)}
-        weight[kt] = jnp.where(row > ks, weight[kt], 0.0)
-        for m in range(k + 1, width):
-            x = spread_row(column[k][m // 8], m % 8)
-            for i in range(m // 8, depth):
-                column[m][i] = column[m][i] - weight[i] * x
-        for c in range(len(tiles[0])):
-            t = spread_row(tiles[kt][c], ks)
-            for i in range(kt + (ks == 7), depth):
-                tiles[i][c] = tiles[i][c] - weight[i] * t
+    for begin in range(0, width, group):
+        column = {}
+        for k in range(begin, begin + group):
+            for i in range(k // 8, depth):
+                column[k, i] = jnp.broadcast_to(
+                    tiles[i][0][:, first + k : first + k + 1], (8, 128)
+                )
+        for k in range(begin, begin + group):
+            kt, ks = k // 8, k % 8
+            pivot = spread_row(column[k, kt], ks)
+            pivots[kt] = jnp.where(row == ks, pivot, pivots[kt])
+            if k == width - 1:
+                break
+            inverse = 1.0 / pivot
+            below = {i: column[k, i] for i in range(kt, depth)}
+            below[kt] = jnp.where(row > ks, below[kt], 0.0)
+            weight = {i: below[i] * inverse for i in below}
+            for m in range(k + 1, begin + group):
+                x = spread_row(column[k, m // 8], m % 8)
+                for i in range(m // 8, depth):
+                    if m == k + 1:
+                        column[m, i] = column[m, i] - (below[i] * x) * inverse
+                    else:
+                        column[m, i] = column[m, i] - weight[i] * x
+            for c in range(len(tiles[0])):
+                t = spread_row(tiles[kt][c], ks)
+                for i in range(kt + (ks == 7), depth):
+                    tiles[i][c] = tiles[i][c] - weight[i] * t
     for i in range(depth):
         scale = lax.rsqrt(pivots[i])
         tiles[i] = [t * scale for t in tiles[i]]
@@ -104,15 +111,21 @@
 
 
 def leverage_kernel(
-    nz, points, own_freq, start, factor_ref, score_ref,
-    freqs, feats, block, part, got_y, sum_y, got_z, all_z, blocks, a_ref, work, inverses,
-    fs, fr, ys, yr, zs, zr, gs, gr, hs, hr, xs, xr,
+    nz, points_in, freq_in, start, factor_ref, score_ref,
+    points, freqs, feats, block, part, got_y, sum_y, got_z, all_z, blocks, a_ref, work, inverses,
+    fs, fr, ys, yr, zs, zr, gs, gr, hs, hr, xs, xr, ps, pr, local,
 ):
     dp, f = lax.axis_index("dp"), lax.axis_index("feat")
     ny, nx, nf = 4, 4, 8
     half_way = nf // 2
     total = 128 * nf
     total_rows = points.shape[0] * nz * ny
+    fetch = [
+        pltpu.make_async_copy(points_in, points, local.at[0]),
+        pltpu.make_async_copy(freq_in, freqs.at[lax.axis_index("feat")], local.at[1]),
+    ]
+    for copy in fetch:
+        copy.start()
     z, y, x, core = dp // ny, dp % ny, f // 2, f % 2
     other = 1 - core
     near = f + 1 - 2 * core
@@ -182,7 +195,7 @@
             part[q, 32 * half_way : 32 * half_way + 16, :] = block[rows, :]
 
     def panel_in(g):
-        send(own_freq, freqs.at[g], fs.at[0], fr.at[g], sibling).wait_recv()
+        send(freqs.at[g], freqs.at[g], fs.at[0], fr.at[g], sibling).wait_recv()
 
     def pass_panel(k):
         g = x_peer[k][1]
@@ -190,7 +203,9 @@
         go(freqs.at[g], freqs.at[g], fs.at[nx + k - 1], fr.at[g], sibling)
         return g
 
-    freqs[f] = own_freq[...]
+    for copy in fetch:
+        copy.wait()
+    own_freq = freqs.at[f]
     pair(f)
     keep(0)
     pl.semaphore_wait(barrier, len(peers))
@@ -236,21 +251,51 @@
             y_copy(k, d).wait_recv()
     sum_y[...] = ((part[y] + got_y[1]) + got_y[2]) + got_y[3]
 
-    slab = 16
-    owners = share // slab
-    own_slab = pl.ds(pl.multiple_of(jnp.minimum(z, owners - 1) * slab, slab), slab)
-
-    def to_owner(owner):
-        at = slice(owner * slab, owner * slab + slab)
+    slab = 8
+    owner_of = [4 * (t % 4) + t // 4 for t in range(16)] + [3, 11]
+
+    def z_copy(t):
+        at = slice(t * slab, t * slab + slab)
+        slot = nz * (t // nz) + z
         return send(
-            sum_y.at[at], got_z.at[z], zs.at[owner], zr.at[z], (owner * ny + y, f)
-        )
-
-    for owner in range(owners):
-
-        @pl.when(z != owner)
+            sum_y.at[at], got_z.at[slot], zs.at[t], zr.at[slot], (owner_of[t] * ny + y, f)
+        )
+
+    for t in range(len(owner_of)):
+
+        @pl.when(z != owner_of[t])
         def _():
-            to_owner(owner).start()
+            z_copy(t).start()
+
+    def collect(t, extra):
+        base = nz * extra
+        at = pl.ds(pl.multiple_of(t * slab, slab), slab)
+        got_z[base + z] = sum_y[at, :]
+        for source in range(nz):
+
+            @pl.when(z != source)
+            def _():
+                send(
+                    sum_y.at[0:slab], got_z.at[base + source], zs.at[0],
+                    zr.at[base + source], z_peer[1],
+                ).wait_recv()
+
+        whole = got_z[base]
+        for source in range(1, nz):
+            whole = whole + got_z[base + source]
+        all_z[at, :] = whole
+        for k in sorted(range(1, nz), key=lambda k: -min(k, nz - k)):
+            spread_z(t, extra, k).start()
+
+    def spread_z(t, extra, k):
+        at = pl.ds(pl.multiple_of(t * slab, slab), slab)
+        return send(
+            all_z.at[at], all_z.at[at], gs.at[nz * extra + k], gr.at[t], z_peer[k]
+        )
+
+    own_tile = (z % 4) * 4 + z // 4
+    extra_tile = 16 + z // 8
+    has_extra = z % 8 == 3
 
     pass_panel(3)
     panel_in(((x + 3) % nx) * 2 + other)
@@ -265,23 +310,11 @@
         )
         a_ref[128 * g : 128 * g + 128, total : total + 128] = scaled_cosine(angle + phase)
 
-    @pl.when(z < owners)
+    collect(own_tile, 0)
+
+    @pl.when(has_extra)
     def _():
-        got_z[z] = sum_y[own_slab, :]
-        for source in range(nz):
-
-            @pl.when(z != source)
-            def _():
-                send(
-                    sum_y.at[0:slab], got_z.at[source], zs.at[0], zr.at[source], z_peer[1]
-                ).wait_recv()
-
-        whole = got_z[0]
-        for source in range(1, nz):
-            whole = whole + got_z[source]
-        all_z[own_slab, :] = whole
-        for k in sorted(range(1, nz), key=lambda k: -min(k, nz - k)):
-            send(all_z.at[own_slab], all_z.at[own_slab], gs.at[k], gr.at[z], z_peer[k]).start()
+        collect(extra_tile, 1)
 
     def gather_y(d, k):
         n = rows_of(d)
@@ -291,19 +324,45 @@
             hs.at[k, d], hr.at[k, d], y_peer[k],
         )
 
-    def spread_y(d):
-        for owner in range(2 * d, min(2 * d + 2, owners)):
-
-            @pl.when(z != owner)
+    def take_z(d):
+        for t in range(4 * d, min(4 * d + 4, len(owner_of))):
+
+            @pl.when(z != owner_of[t])
             def _():
-                at = slice(owner * slab, owner * slab + slab)
-                send(all_z.at[at], all_z.at[at], gs.at[1], gr.at[owner], z_peer[1]).wait_recv()
+                at = slice(t * slab, t * slab + slab)
+                send(all_z.at[at], all_z.at[at], gs.at[1], gr.at[t], z_peer[1]).wait_recv()
 
         n = rows_of(d)
         mine = pl.ds(pl.multiple_of(128 * d + n * y, 16), n)
         blocks[f, mine, :] = all_z[32 * d : 32 * d + n, :]
+
+    def spread_y(d):
+        take_z(d)
         for k in range(1, ny):
             gather_y(d, k).start()
+
+    plane = [(i, k) for i in range(nx) for k in range(ny) if (i, k) != (0, 0)]
+
+    def plane_copy(i, k, back):
+        xx, yy = (x + nx - i) % nx if back else x, (y + ny - k) % ny if back else y
+        rows = blocks.at[xx * 2 + core, pl.ds(pl.multiple_of(32 * yy, 32), 32)]
+        to = (z * ny + (y + k) % ny, ((x + i) % nx) * 2 + core)
+        return send(rows, rows, ps.at[i * ny + k], pr.at[i * ny + k], to)
+
+    def first_round():
+        take_z(0)
+        for i, k in sorted(plane, key=lambda p: -min(p[0], 4 - p[0]) - min(p[1], 4 - p[1])):
+            plane_copy(i, k, False).start()
+
+    def first_round_in():
+        for i in (0, 1, 3, 2):
+            for k in range(ny):
+                if (i, k) != (0, 0):
+                    plane_copy(i, k, True).wait_recv()
+            g = ((x + nx - i) % nx) * 2 + core
+            round_copy(g, 0, i, sibling).start()
+        for i in range(nx):
+            round_copy(((x + nx - i) % nx) * 2 + other, 0, 0, sibling).wait_recv()
 
     def round_copy(g, d, k, to):
         piece = blocks.at[g, 128 * d : 128 * d + 4 * rows_of(d)]
@@ -363,14 +422,11 @@
         work[:, 0:128] = a_ref[r : r + 128, r : r + 128]
         work[:, 128:256] = eye
 
-    spread_y(0)
-    round_out(0)
+    first_round()
     for d in range(1, half_way + 1):
         spread_y(d)
-    for k in (3, 2, 1):
-        round_copy(f, 0, k, x_peer[k]).wait_send()
     round_out(1)
-    round_in(0)
+    first_round_in()
     load(0, 0)
     begin(0)
     round_out(2)
@@ -414,20 +470,25 @@
     for d in range(half_way + 1):
         for k in range(1, ny):
             y_copy(k, d).wait_send()
-            gather_y(d, k).wait_send()
-        for k in range(7):
-            if d > 0 or k not in (1, 2, 3):
-                round_copy(f, d, k, sibling).wait_send()
-    for owner in range(owners):
-
-        @pl.when(z != owner)
+            if d:
+                gather_y(d, k).wait_send()
+        for k in range(7 if d else 4):
+            round_copy(f, d, k, sibling).wait_send()
+    for i, k in plane:
+        plane_copy(i, k, False).wait_send()
+    for t in range(len(owner_of)):
+
+        @pl.when(z != owner_of[t])
         def _():
-            to_owner(owner).wait_send()
-
-    @pl.when(z < owners)
+            z_copy(t).wait_send()
+
+    for k in range(1, nz):
+        spread_z(own_tile, 0, k).wait_send()
+
+    @pl.when(has_extra)
     def _():
         for k in range(1, nz):
-            send(all_z.at[own_slab], all_z.at[own_slab], gs.at[k], gr.at[z], z_peer[k]).wait_send()
+            spread_z(extra_tile, 1, k).wait_send()
 
 
 def per_device(points, frequencies, halton_start):
@@ -445,26 +506,32 @@
             jax.ShapeDtypeStruct((total, 128), f32),
             jax.ShapeDtypeStruct((1, 128), f32),
         ),
-        in_specs=[in_vmem, in_vmem, pl.BlockSpec(memory_space=pltpu.SMEM)],
+        in_specs=[
+            pl.BlockSpec(memory_space=pltpu.HBM),
+            pl.BlockSpec(memory_space=pltpu.HBM),
+            pl.BlockSpec(memory_space=pltpu.SMEM),
+        ],
         out_specs=(in_vmem,) * 2,
         scratch_shapes=[
+            pltpu.VMEM((rows, dim), f32),
             pltpu.VMEM((nf, dim, 128), f32),
             pltpu.VMEM((nf, rows, 128), f32),
             pltpu.VMEM((128, 128), f32),
             pltpu.VMEM((4, share, 128), f32),
             pltpu.VMEM((4, share, 128), f32),
             pltpu.VMEM((share, 128), f32),
-            pltpu.VMEM((nz, 16, 128), f32),
+            pltpu.VMEM((2 * nz, 8, 128), f32),
             pltpu.VMEM((share, 128), f32),
             pltpu.VMEM((nf, 4 * share, 128), f32),
             pltpu.VMEM((total, total + 128), f32),
             pltpu.VMEM((128, 256), f32),
             pltpu.VMEM((nf, 128, 128), f32),
-            dma((8,)), dma((nf,)), dma((20,)), dma((20,)), dma((nz,)), dma((nz,)),
-            dma((nz,)), dma((nz,)), dma((4, 5)), dma((4, 5)), dma((8, 5)), dma((5 * nf,)),
+            dma((8,)), dma((nf,)), dma((20,)), dma((20,)), dma((18,)), dma((2 * nz,)),
+            dma((2 * nz,)), dma((18,)), dma((4, 5)), dma((4, 5)), dma((8, 5)), dma((5 * nf,)),
+            dma((16,)), dma((16,)), dma((2,)),
         ],
         compiler_params=pltpu.CompilerParams(
-            vmem_limit_bytes=48 * 2**20, collective_id=0, has_side_effects=True
+            vmem_limit_bytes=63 * 2**20, collective_id=0, has_side_effects=True
         ),
     )(points, frequencies, halton_start)
     return (scores.reshape(128), own_factor)

time: 110 us -> 106 us (0.964)
  Pallas kernels: 105 us -> 101 us
    pallas_call x1, Pallas kernels: 105 us -> 101 us  [per_device(): pl.pallas_call(functools.partial(leverage_kernel, nz), out_shape=(jax.Sha...]
    unnamed x6 -> x4, local copies, waits for them, and re-layouts: 3.43 us -> 3.04 us
where the time goes in v5:
time: 106 us; the launch traced here: 105 us
  Pallas kernels  101 us (95%)
  local copies, waits for them, and re-layouts  3.04 us (3%)
  between operations  1.29 us (1%)
    pallas_call x1, Pallas kernels, per_device(): pl.pallas_call(functools.partial(leverage_kernel, nz), out_shape=(jax.Sha...  101 us
    unnamed x4, local copies, waits for them, and re-layouts  3.04 us

profile of v5, /device:TPU:1, one launch (start us, length us, event | category | flops | bytes accessed | tf_op | source)
XLA Modules:
  0.0 105.5 jit_solution(7019960476105605989)
XLA Ops:
  1.3 101.1 %shard_map.50 = (f32[1024,128]{1,0:T(8,128)}, f32[1,128]{1,0:T(1,128)}) custom-call(f32[1024,256]{1,0:T(8,128)} %points_in.1, f32[256,128]{1,0:T(8,128)} %freq_in.1, s32[1]{0:T(128)S(6)} %copy.7.start), custom_call_target="tpu_custom_call" | custom-call | tf_op jit(solution)/shard_map/pallas_call | solution.py:503
  102.4 0.0 copy-start
  102.4 0.7 copy-done
  103.1 0.5 copy.8
  103.6 1.9 %copy.9 = f32[1024,128]{1,0:T(8,128)} copy(f32[1024,128]{1,0:T(8,128)} %get-tuple-element.9) | data formatting | bytes 1048576
Async XLA Ops:
  102.4 0.7 copy-start

commit v6 on v5

--- a/solution.py
+++ b/solution.py
@@ -19,6 +19,12 @@
 def gram_of(left, right):
     return lax.dot_general(
         left, right, (((0,), (0,)), ((), ())), precision=HI, preferred_element_type=jnp.float32
+    )
+
+
+def half_gram(left, right):
+    return lax.dot_general(
+        left, right, (((0,), (0,)), ((), ())), preferred_element_type=jnp.float32
     )
 
 
@@ -88,15 +94,13 @@
 TURN_HIGH = 6.28125
 TURN_LOW = 2.0 * math.pi - TURN_HIGH
 COSINE = (
-    1.4142135623717025,
-    -0.7071067811637958,
-    0.058925565037607174,
-    -0.0019641854397455995,
-    3.507470808988151e-05,
-    -3.897096847328774e-07,
-    2.950756124473042e-09,
-    -1.6054447590940767e-11,
-    5.837442578648932e-14,
+    1.4142135468607229,
+    -0.7071066265100442,
+    0.05892531321284991,
+    -0.0019640314894530655,
+    3.502977695707701e-05,
+    -3.8294155634471805e-07,
+    2.438284561288029e-09,
 )
 
 
@@ -112,7 +116,7 @@
 
 def leverage_kernel(
     nz, points_in, freq_in, start, factor_ref, score_ref,
-    points, freqs, feats, block, part, got_y, sum_y, got_z, all_z, blocks, a_ref, work, inverses,
+    points, freqs, feats, rests, block, part, got_y, sum_y, got_z, all_z, blocks, a_ref, work, inverses,
     fs, fr, ys, yr, zs, zr, gs, gr, hs, hr, xs, xr, ps, pr, local,
 ):
     dp, f = lax.axis_index("dp"), lax.axis_index("feat")
@@ -163,12 +167,17 @@
             angle = jnp.dot(
                 points[rows, :], freqs[g], precision=HI, preferred_element_type=jnp.float32
             )
-            feats[g, rows, :] = scaled_cosine(angle + phase)
+            value = scaled_cosine(angle + phase)
+            coarse = value.astype(jnp.bfloat16)
+            feats[g, rows, :] = coarse
+            rests[g, rows, :] = (value - coarse.astype(jnp.float32)).astype(jnp.bfloat16)
 
     def pair(g):
         featurize(g)
         low, high = jnp.minimum(f, g), jnp.maximum(f, g)
-        block[...] = gram_of(feats[low], feats[high])
+        a, b, c, d = feats[low], rests[low], feats[high], rests[high]
+        small = (half_gram(a, d) + half_gram(b, c)) + half_gram(b, d)
+        block[...] = half_gram(a, c) + small
 
     def keep(d):
         at = pl.ds(32 * d if isinstance(d, int) else pl.multiple_of(32 * d, 32), 32)
@@ -433,7 +442,7 @@
 
     @pl.loop(0, nf)
     def _(p):
-        factor_diagonal(work, 32)
+        factor_diagonal(work, 64)
         inverses[p] = work[:, 128:256]
         for k in range(nf):
 
@@ -515,7 +524,8 @@
         scratch_shapes=[
             pltpu.VMEM((rows, dim), f32),
             pltpu.VMEM((nf, dim, 128), f32),
-            pltpu.VMEM((nf, rows, 128), f32),
+            pltpu.VMEM((nf, rows, 128), jnp.bfloat16),
+            pltpu.VMEM((nf, rows, 128), jnp.bfloat16),
             pltpu.VMEM((128, 128), f32),
             pltpu.VMEM((4, share, 128), f32),
             pltpu.VMEM((4, share, 128), f32),
@@ -531,9 +541,13 @@
             dma((16,)), dma((16,)), dma((2,)),
         ],
         compiler_params=pltpu.CompilerParams(
-            vmem_limit_bytes=63 * 2**20, collective_id=0, has_side_effects=True
+            vmem_limit_bytes=48 * 2**20, collective_id=0, has_side_effects=True
         ),
-    )(points, frequencies, halton_start)
+    )(
+        pltpu.with_memory_space_constraint(points, pltpu.HBM),
+        pltpu.with_memory_space_constraint(frequencies, pltpu.HBM),
+        halton_start,
+    )
     return (scores.reshape(128), own_factor)
 
 

time: 106 us -> 103 us (0.972)
  local copies, waits for them, and re-layouts: 3.04 us -> 1.31 us
    unnamed x4 -> x2, local copies, waits for them, and re-layouts: 3.04 us -> 1.31 us
where the time goes in v6:
time: 103 us
  Pallas kernels  100 us (97%)
  local copies, waits for them, and re-layouts  1.31 us (1%)
  between operations  1.29 us (1%)
    pallas_call x1, Pallas kernels, per_device(): pl.pallas_call(functools.partial(leverage_kernel, nz), out_shape=(jax.Sha...  100 us

profile of v6, /device:TPU:1, one launch (start us, length us, event | category | flops | bytes accessed | tf_op | source)
XLA Modules:
  0.0 102.8 jit_solution(13693315172265163065)
XLA Ops:
  1.3 100.2 %shard_map.50 = (f32[1024,128]{1,0:T(8,128)S(1)}, f32[1,128]{1,0:T(1,128)S(1)}) custom-call(f32[1024,256]{1,0:T(8,128)} %points_in.1, f32[256,128]{1,0:T(8,128)} %freq_in.1, s32[1]{0:T(128)S(6)} %copy.7.start), custom_call_target="tpu_custom_call" | custom-call | tf_op jit(solution)/shard_map/pallas_call | solution.py:512
  101.5 0.5 copy.8
  102.0 0.8 copy.9

commit v7 on v6

--- a/solution.py
+++ b/solution.py
@@ -212,15 +212,15 @@
         go(freqs.at[g], freqs.at[g], fs.at[nx + k - 1], fr.at[g], sibling)
         return g
 
-    for copy in fetch:
-        copy.wait()
+    fetch[1].wait()
     own_freq = freqs.at[f]
-    pair(f)
-    keep(0)
     pl.semaphore_wait(barrier, len(peers))
     go(own_freq, freqs.at[f], fs.at[0], fr.at[f], sibling)
     for k in (3, 2):
         go(own_freq, freqs.at[f], fs.at[k], fr.at[f], x_peer[k])
+    fetch[0].wait()
+    pair(f)
+    keep(0)
     pass_on(0)
 
     panel_in(near)
@@ -432,12 +432,13 @@
         work[:, 128:256] = eye
 
     first_round()
-    for d in range(1, half_way + 1):
+    for d in range(1, half_way):
         spread_y(d)
     round_out(1)
     first_round_in()
     load(0, 0)
     begin(0)
+    spread_y(half_way)
     round_out(2)
 
     @pl.loop(0, nf)

time: 103 us -> 102 us (level)
    pallas_call x1, Pallas kernels: 100 us -> 99.1 us  [per_device(): pl.pallas_call(functools.partial(leverage_kernel, nz), out_shape=(jax.Sha...]
where the time goes in v7:
time: 102 us
  Pallas kernels  99.1 us (97%)
  local copies, waits for them, and re-layouts  1.31 us (1%)
  between operations  1.29 us (1%)
    pallas_call x1, Pallas kernels, per_device(): pl.pallas_call(functools.partial(leverage_kernel, nz), out_shape=(jax.Sha...  99.1 us

profile of v7, /device:TPU:1, one launch (start us, length us, event | category | flops | bytes accessed | tf_op | source)
XLA Modules:
  0.0 101.7 jit_solution(7740768842701861358)
XLA Ops:
  1.3 99.1 %shard_map.50 = (f32[1024,128]{1,0:T(8,128)S(1)}, f32[1,128]{1,0:T(1,128)S(1)}) custom-call(f32[1024,256]{1,0:T(8,128)} %points_in.1, f32[256,128]{1,0:T(8,128)} %freq_in.1, s32[1]{0:T(128)S(6)} %copy.7.start), custom_call_target="tpu_custom_call" | custom-call | tf_op jit(solution)/shard_map/pallas_call | solution.py:513
  100.4 0.5 copy.8
  100.9 0.8 copy.9
